TPU v7x, 128 devices: a whole 4x4x4 slice. The times are simulated.
128 devices in a mesh: expert: 32 (over z, x, core), dp: 4 (over y).
Axes of the slice: x: 4, y: 4, z: 4, core: 2. Of those that a mesh axis runs over, the one named last changes fastest.
Arguments:
- tokens: bfloat16 [8192, 2048], P(('expert', 'dp')), may hold values from -6 to 6
- routes: int32 [8192, 8], P(('expert', 'dp')), may hold values from 0 to 127, all different within a row; in each aligned block of 64 rows (0 to 63, 64 to 127, ...) at most 5 rows name the same one
- probs: float32 [8192, 8], P(('expert', 'dp')), may hold values from 0.02 to 1
- cotangent: bfloat16 [8192, 2048], P(('expert', 'dp')), may hold values from -6 to 6
- w_gate: bfloat16 [128, 2048, 384], P('expert'), may hold values from -0.125 to 0.125
- w_up: bfloat16 [128, 2048, 384], P('expert'), may hold values from -0.125 to 0.125
- w_down: bfloat16 [128, 2048, 384], P('expert'), may hold values from -0.3125 to 0.3125
Outputs:
- mixed: bfloat16 [8192, 2048], P(('expert', 'dp'))
- token_grad: bfloat16 [8192, 2048], P(('expert', 'dp'))
- prob_grad: float32 [8192, 8], P(('expert', 'dp'))
- gate_grad: bfloat16 [128, 2048, 384], P('expert', 'dp')
- up_grad: bfloat16 [128, 2048, 384], P('expert', 'dp')
- down_grad: bfloat16 [128, 2048, 384], P('expert', 'dp')
Inputs may be any that keep to these rules, and one draw needn't show every extreme that they name: `routes`: each row names 8 different experts. Among the 64 rows of one device no expert is named by more than 5 rows, a bound that some block reaches.
All inputs are finite; a program needn't handle non-finite values.
Results may differ from a plain program's by a relative error of at most 0.0095.
Values may be sent and summed in bfloat16 or wider, within the bound.
A program may use at most 128 MiB of HBM per device.

v0:
```python
import jax
import jax.numpy as jnp
from jax import lax
from jax.sharding import PartitionSpec as P


def expert_forward(rows_in, w_gate, w_up, w_down):
    gate_pre = jnp.einsum("krd,kdh->krh", rows_in, w_gate, preferred_element_type=jnp.float32)
    up_pre = jnp.einsum("krd,kdh->krh", rows_in, w_up, preferred_element_type=jnp.float32)
    sigmoid_gate = jax.nn.sigmoid(gate_pre)
    active = (gate_pre * sigmoid_gate * up_pre).astype(jnp.bfloat16)
    output = jnp.einsum("krh,kdh->krd", active, w_down, preferred_element_type=jnp.float32).astype(
        jnp.bfloat16
    )
    return ((gate_pre, up_pre, sigmoid_gate, active), output)


def expert_backward(rows_in, upstream, saved_state, w_gate, w_up, w_down):
    gate_pre, up_pre, sigmoid_gate, active = saved_state
    d_active = jnp.einsum("krd,kdh->krh", upstream, w_down, preferred_element_type=jnp.float32)
    grad_down = jnp.einsum("krd,krh->kdh", upstream, active, preferred_element_type=jnp.float32)
    d_gate = (d_active * up_pre * sigmoid_gate * (1.0 + gate_pre * (1.0 - sigmoid_gate))).astype(
        jnp.bfloat16
    )
    d_up = (d_active * gate_pre * sigmoid_gate).astype(jnp.bfloat16)
    d_input = (
        jnp.einsum("krh,kdh->krd", d_gate, w_gate, preferred_element_type=jnp.float32)
        + jnp.einsum("krh,kdh->krd", d_up, w_up, preferred_element_type=jnp.float32)
    ).astype(jnp.bfloat16)
    grad_gate = jnp.einsum("krd,krh->kdh", rows_in, d_gate, preferred_element_type=jnp.float32)
    grad_up = jnp.einsum("krd,krh->kdh", rows_in, d_up, preferred_element_type=jnp.float32)
    gate_part, up_part, down_part = (
        lax.psum_scatter(
            grad_gate.astype(jnp.bfloat16), "dp", scatter_dimension=1, tiled=True
        ).astype(jnp.float32),
        lax.psum_scatter(
            grad_up.astype(jnp.bfloat16), "dp", scatter_dimension=1, tiled=True
        ).astype(jnp.float32),
        lax.psum_scatter(
            grad_down.astype(jnp.bfloat16), "dp", scatter_dimension=1, tiled=True
        ).astype(jnp.float32),
    )
    return (d_input, (gate_part, up_part, down_part))


def shards(tokens, routes, probs, cotangent, w_gate, w_up, w_down):
    tok_rows, top_count = routes.shape
    model_width = tokens.shape[1]
    local_count = w_gate.shape[0]
    peer_count = lax.axis_size("expert")
    experts_all = local_count * peer_count
    capacity = 5 * tok_rows * top_count // (4 * experts_all)
    slot_count = local_count * peer_count * capacity
    entry_count = tok_rows * top_count
    buffer_shape = (local_count, peer_count, capacity, model_width)
    flat_shape = (local_count, peer_count * capacity, model_width)
    flat_expert = routes.reshape(-1)
    expert_range = jnp.arange(experts_all, dtype=jnp.int32)
    onehot_table = (flat_expert[:, None] == expert_range[None, :]).astype(jnp.int32)
    slot_rank = jnp.sum((jnp.cumsum(onehot_table, axis=0) - 1) * onehot_table, axis=1)
    owner_dev = flat_expert // local_count
    local_index = flat_expert % local_count
    target = (local_index * peer_count + owner_dev) * capacity + slot_rank
    source = (
        jnp.zeros((slot_count,), jnp.int32)
        .at[target]
        .set(jnp.arange(entry_count, dtype=jnp.int32) + 1)
    )
    filled = (source > 0)[:, None]
    pick_index = jnp.maximum(source - 1, 0)
    token_index = pick_index // top_count
    totals = jnp.sum(probs, axis=1, keepdims=True)
    gate_share = probs / totals
    shares_flat = gate_share.reshape(-1)
    zero_value = jnp.zeros((), jnp.bfloat16)
    send_inputs = jnp.where(filled, tokens[token_index], zero_value).reshape(buffer_shape)
    scaled = (shares_flat[pick_index][:, None] * cotangent[token_index].astype(jnp.float32)).astype(
        jnp.bfloat16
    )
    send_upstream = jnp.where(filled, scaled, zero_value).reshape(buffer_shape)
    recv_inputs, recv_upstream = (
        lax.all_to_all(send_inputs, "expert", split_axis=1, concat_axis=1, tiled=True),
        lax.all_to_all(send_upstream, "expert", split_axis=1, concat_axis=1, tiled=True),
    )
    recv_inputs = recv_inputs.reshape(flat_shape)
    recv_upstream = recv_upstream.reshape(flat_shape)
    saved_state, output = expert_forward(recv_inputs, w_gate, w_up, w_down)
    d_input, weight_parts = expert_backward(
        recv_inputs, recv_upstream, saved_state, w_gate, w_up, w_down
    )
    back_output, back_input = (
        lax.all_to_all(
            output.reshape(buffer_shape), "expert", split_axis=1, concat_axis=1, tiled=True
        ),
        lax.all_to_all(
            d_input.reshape(buffer_shape), "expert", split_axis=1, concat_axis=1, tiled=True
        ),
    )
    out_rows = back_output.reshape(slot_count, model_width)[target].reshape(
        tok_rows, top_count, model_width
    )
    grad_rows = back_input.reshape(slot_count, model_width)[target].reshape(
        tok_rows, top_count, model_width
    )
    mixed_out = jnp.sum(gate_share[:, :, None] * out_rows.astype(jnp.float32), axis=1).astype(
        jnp.bfloat16
    )
    token_grad = jnp.sum(grad_rows.astype(jnp.float32), axis=1).astype(jnp.bfloat16)
    share_grad = jnp.einsum("tjd,td->tj", out_rows, cotangent, preferred_element_type=jnp.float32)
    prob_grad = (share_grad - jnp.sum(gate_share * share_grad, axis=1, keepdims=True)) / totals
    gate_part, up_part, down_part = weight_parts
    return (
        mixed_out,
        token_grad,
        prob_grad,
        gate_part.astype(jnp.bfloat16),
        up_part.astype(jnp.bfloat16),
        down_part.astype(jnp.bfloat16),
    )


def solution(mesh):
    return jax.shard_map(
        shards,
        mesh=mesh,
        in_specs=(
            P(("expert", "dp"), None),
            P(("expert", "dp"), None),
            P(("expert", "dp"), None),
            P(("expert", "dp"), None),
            P("expert", None, None),
            P("expert", None, None),
            P("expert", None, None),
        ),
        out_specs=(
            P(("expert", "dp"), None),
            P(("expert", "dp"), None),
            P(("expert", "dp"), None),
            P("expert", "dp", None),
            P("expert", "dp", None),
            P("expert", "dp", None),
        ),
        check_vma=False,
    )
```

profile of v0, /device:TPU:7, one launch (start us, length us, event | category | flops | bytes accessed | tf_op | source)
XLA Modules:
  0.0 395.2 jit_solution(3304004591598301683)
XLA Ops:
  11.8 3.4 gather_fusion
  20.9 2.9 copy.39
  23.8 41.7 %all_to_all.20 = bf16[4,32,5,2048]{3,0,2,1:T(4,128)(2,1)S(1)} all-to-all(bf16[4,32,5,2048]{3,0,2,1:T(4,128)(2,1)S(1)} %copy.39), channel_id=1, replica_groups=mesh['expert'=32,'dp'=4] {'expert'}, dimensions={1} | all-to-all | bytes 5242880 | tf_op jit(solution)/shard_map/all_to_all | solution.py:82
  65.5 3.8 fusion.10
  69.4 4.7 %multiply_convert_fusion.3 = (bf16[4,160,384]{2,1,0:T(8,128)(2,1)S(1)}, f32[4,160,384]{2,1,0:T(8,128)}) fusion(f32[4,160,384]{2,1,0:T(8,128)S(1)} %fusion.10, bf16[4,2048,384]{2,1,0:T(8,128)(2,1)S(1)} %bitcast.53, bf16[4,160,2048]{2,0,1:T(4,128)(2,1)S(1)} %bitcast.43), kind=kOutput, calls=%fused_computation.29 | convolution fusion | flops 1008107520 | bytes 11370496 | tf_op jit(solution)/shard_map/krd,kdh->krh/dot_general | solution.py:9
  76.3 3.6 copy.42
  79.8 5.3 %all-to-all-start.1 = ((bf16[4,32,5,2048]{3,0,2,1:T(4,128)(2,1)}), bf16[4,32,5,2048]{3,0,2,1:T(4,128)(2,1)S(1)}, u32[]{:S(2)}, u32[]{:S(2)}) async-start(bf16[4,32,5,2048]{3,0,2,1:T(4,128)(2,1)} %bitcast.48), calls=%async_computation.1 | async-start | bytes 5242880 | tf_op jit(solution)/shard_map/all_to_all | solution.py:92
  85.7 4.1 %gather_fusion.3 = bf16[640,2048]{1,0:T(8,128)(2,1)} fusion(bf16[64,2048]{1,0:T(8,128)(2,1)S(1)} %copy-done, s32[1024]{0:T(1024)S(1)} %get-tuple-element.15), kind=kCustom, calls=%fused_computation.3 | custom fusion | bytes 5245440 | tf_op jit(solution)/shard_map/gather | solution.py:77
  89.8 5.9 %reshape.217 = f32[4,32,5,2048]{3,2,1,0:T(8,128)} reshape(bf16[640,2048]{1,0:T(8,128)(2,1)} %gather_fusion.3) | data formatting | bytes 7864320 | tf_op jit(solution)/shard_map/convert_element_type | solution.py:77
  95.7 22.4 %all-to-all-done.1 = bf16[4,32,5,2048]{3,0,2,1:T(4,128)(2,1)S(1)} async-done(((bf16[4,32,5,2048]{3,0,2,1:T(4,128)(2,1)}), bf16[4,32,5,2048]{3,0,2,1:T(4,128)(2,1)S(1)}, u32[]{:S(2)}, u32[]{:S(2)}) %all-to-all-start.1) | async-done | bytes 2621472 | tf_op jit(solution)/shard_map/all_to_all | solution.py:92
  118.2 3.4 copy.43
  121.6 4.2 %reshape.210 = bf16[640,2048]{1,0:T(8,128)(2,1)S(1)} reshape(bf16[4,32,5,2048]{3,2,1,0:T(8,128)(2,1)} %copy.43) | data formatting | bytes 5242880 | tf_op jit(solution)/shard_map/reshape | solution.py:99
  125.8 3.3 gather_fusion.1
  129.1 3.0 fusion.4
  132.4 4.3 %gather_fusion.2 = f32[640]{0:T(1024)S(1)} fusion(f32[512]{0:T(512)S(1)} %reshape.212, s32[1024]{0:T(1024)S(1)} %get-tuple-element.14), kind=kCustom, calls=%fused_computation.2 | custom fusion | bytes 7680 | tf_op jit(solution)/shard_map/gather | solution.py:77
  136.9 3.9 fusion
  143.7 39.2 %all_to_all.21 = bf16[4,32,5,2048]{3,0,2,1:T(4,128)(2,1)S(1)} all-to-all(bf16[4,32,5,2048]{3,0,2,1:T(4,128)(2,1)S(1)} %copy.45), channel_id=1, replica_groups=mesh['expert'=32,'dp'=4] {'expert'}, dimensions={1} | all-to-all | bytes 5242880 | tf_op jit(solution)/shard_map/all_to_all | solution.py:83
  184.5 7.6 %convolution_convert_fusion = bf16[4,2048,384]{2,1,0:T(8,128)(2,1)} fusion(bf16[4,160,384]{2,1,0:T(8,128)(2,1)S(1)} %get-tuple-element.12, bf16[4,160,2048]{2,0,1:T(4,128)(2,1)S(1)} %bitcast.50), kind=kOutput, calls=%fused_computation.8 | convolution fusion | flops 1009778688 | bytes 9404416 | tf_op jit(solution)/shard_map/krd,krh->kdh/dot_general | solution.py:21
  192.1 7.9 %multiply_convert_fusion.1 = (bf16[4,160,384]{2,1,0:T(8,128)(2,1)S(1)}, bf16[4,160,384]{2,1,0:T(8,128)(2,1)S(1)}) fusion(f32[4,160,384]{2,1,0:T(8,128)} %copy-done.9, f32[4,160,384]{2,1,0:T(8,128)} %get-tuple-element.13, bf16[4,2048,384]{2,1,0:T(8,128)(2,1)} %param.13, bf16[4,160,2048]{2,0,1:T(4,128)(2,1)} %bitcast.51), kind=kOutput, calls=%fused_computation.27 | convolution fusion | flops 1009827840 | bytes 11862016 | tf_op jit(solution)/shard_map/krd,kdh->krh/dot_general | solution.py:20
  200.8 7.5 %convolution_convert_fusion.1 = bf16[4,2048,384]{2,1,0:T(8,128)(2,1)} fusion(bf16[4,160,384]{2,1,0:T(8,128)(2,1)S(1)} %get-tuple-element.8, bf16[4,160,2048]{2,0,1:T(4,128)(2,1)S(1)} %bitcast.44), kind=kOutput, calls=%fused_computation.9 | convolution fusion | flops 1009778688 | bytes 9404416 | tf_op jit(solution)/shard_map/krd,krh->kdh/dot_general | solution.py:31
  208.6 7.6 %convolution_convert_fusion.2 = bf16[4,2048,384]{2,1,0:T(8,128)(2,1)} fusion(bf16[4,160,384]{2,1,0:T(8,128)(2,1)S(1)} %get-tuple-element.9, bf16[4,160,2048]{2,0,1:T(4,128)(2,1)S(1)} %bitcast.45), kind=kOutput, calls=%fused_computation.10 | convolution fusion | flops 1009778688 | bytes 9404416 | tf_op jit(solution)/shard_map/krd,krh->kdh/dot_general | solution.py:30
  216.2 5.2 %fusion.24 = f32[4,160,2048]{2,1,0:T(8,128)S(1)} fusion(bf16[4,160,384]{2,1,0:T(8,128)(2,1)S(1)} %get-tuple-element.9, bf16[4,2048,384]{2,1,0:T(8,128)(2,1)} %param.11), kind=kOutput, calls=%fused_computation.67 | convolution fusion | flops 1006632960 | bytes 12025856 | tf_op jit(solution)/shard_map/krh,kdh->krd/dot_general | solution.py:27
  223.7 3.5 copy.47
  227.2 5.7 %all-to-all-start.3 = ((bf16[4,32,5,2048]{3,0,2,1:T(4,128)(2,1)}), bf16[4,32,5,2048]{3,0,2,1:T(4,128)(2,1)S(1)}, u32[]{:S(2)}, u32[]{:S(2)}) async-start(bf16[4,32,5,2048]{3,0,2,1:T(4,128)(2,1)} %bitcast.49), calls=%async_computation.3 | async-start | bytes 5242880 | tf_op jit(solution)/shard_map/all_to_all | solution.py:95
  233.5 4.2 %multiply_reduce_fusion = bf16[64,2048]{1,0:T(8,128)(2,1)} fusion(bf16[512,2048]{1,0:T(8,128)(2,1)} %gather_fusion.1, f32[64,8]{1,0:T(8,128)S(1)} %copy.33), kind=kLoop, calls=%fused_computation.12 | loop fusion | flops 3014656 | bytes 2361344 | tf_op jit(solution)/shard_map/reduce_sum | solution.py:105
  237.7 28.0 %all-to-all-done.3 = bf16[4,32,5,2048]{3,0,2,1:T(4,128)(2,1)S(1)} async-done(((bf16[4,32,5,2048]{3,0,2,1:T(4,128)(2,1)}), bf16[4,32,5,2048]{3,0,2,1:T(4,128)(2,1)S(1)}, u32[]{:S(2)}, u32[]{:S(2)}) %all-to-all-start.3) | async-done | bytes 2621472 | tf_op jit(solution)/shard_map/all_to_all | solution.py:95
  265.8 3.5 copy.48
  269.3 4.2 %reshape.215 = bf16[640,2048]{1,0:T(8,128)(2,1)S(1)} reshape(bf16[4,32,5,2048]{3,2,1,0:T(8,128)(2,1)} %copy.48) | data formatting | bytes 5242880 | tf_op jit(solution)/shard_map/reshape | solution.py:102
  273.5 3.3 gather_fusion.4
  276.8 3.7 bitcast_reduce_fusion
  280.5 41.0 %reduce-scatter.6.cloned.1.call-done = bf16[4,512,384]{2,1,0:T(8,128)(2,1)} async-done(((bf16[4,2048,384]{2,1,0:T(8,128)(2,1)}), bf16[4,512,384]{2,1,0:T(8,128)(2,1)}) %reduce-scatter.6.cloned.1.call-update) | async-done | bytes 1572880 | tf_op jit(solution)/shard_map/reduce_scatter | solution.py:36
  321.5 66.7 %reduce-scatter.4.cloned.1.call-done = bf16[4,512,384]{2,1,0:T(8,128)(2,1)} async-done(((bf16[4,2048,384]{2,1,0:T(8,128)(2,1)}), bf16[4,512,384]{2,1,0:T(8,128)(2,1)}) %reduce-scatter.4.cloned.1.call-update) | async-done | bytes 1572880 | tf_op jit(solution)/shard_map/reduce_scatter | solution.py:33
  (79 shorter events, 21.8 us)
Async XLA Ops:
  7.2 78.5 %copy-start = (bf16[64,2048]{1,0:T(8,128)(2,1)S(1)}, bf16[64,2048]{1,0:T(8,128)(2,1)}, u32[]{:S(2)}) copy-start(bf16[64,2048]{1,0:T(8,128)(2,1)} %param.10) | copy-start | bytes 786436
  7.2 4.6 %copy-start.2 = (bf16[64,2048]{1,0:T(8,128)(2,1)S(1)}, bf16[64,2048]{1,0:T(8,128)(2,1)}, u32[]{:S(2)}) copy-start(bf16[64,2048]{1,0:T(8,128)(2,1)} %param.7) | copy-start | bytes 786436
  18.1 47.4 %slice-start = ((s8[6291456]{0:T(1024)(128)(4,1)}), s8[4194304]{0:T(1024)(128)(4,1)S(1)}, s32[]{:S(2)}) async-start(s8[6291456]{0:T(1024)(128)(4,1)} %bitcast.46), calls=%async_computation.10 | async-start | bytes 8388608
  20.9 44.6 %slice-start.1 = ((s8[6291456]{0:T(1024)(128)(4,1)}), s8[2097152]{0:T(1024)(128)(4,1)S(1)}, s32[]{:S(2)}) async-start(s8[6291456]{0:T(1024)(128)(4,1)} %bitcast.46), calls=%async_computation.11 | async-start | bytes 4194304
  23.8 45.5 %slice-start.2 = ((s8[6291456]{0:T(1024)(128)(4,1)}), s8[4194304]{0:T(1024)(128)(4,1)S(1)}, s32[]{:S(2)}) async-start(s8[6291456]{0:T(1024)(128)(4,1)} %bitcast.52), calls=%async_computation.12 | async-start | bytes 8388608
  65.5 3.8 copy-start.3
  65.5 3.8 slice-start.3
  65.5 8.5 %slice-start.6 = ((s8[6291456]{0:T(1024)(128)(4,1)}), s8[2097152]{0:T(1024)(128)(4,1)S(1)}, s32[]{:S(2)}) async-start(s8[6291456]{0:T(1024)(128)(4,1)} %bitcast.56), calls=%async_computation.16 | async-start | bytes 4194304
  69.3 4.7 %copy-start.9 = (f32[4,160,384]{2,1,0:T(8,128)}, f32[4,160,384]{2,1,0:T(8,128)S(1)}, u32[]{:S(2)}) copy-start(f32[4,160,384]{2,1,0:T(8,128)S(1)} %fusion.10) | copy-start | bytes 2949124
  69.3 4.7 %slice-start.7 = ((s8[6291456]{0:T(1024)(128)(4,1)}), s8[4194304]{0:T(1024)(128)(4,1)S(1)}, s32[]{:S(2)}) async-start(s8[6291456]{0:T(1024)(128)(4,1)} %bitcast.56), calls=%async_computation.17 | async-start | bytes 8388608
  79.8 38.3 %all-to-all-start.1 = ((bf16[4,32,5,2048]{3,0,2,1:T(4,128)(2,1)}), bf16[4,32,5,2048]{3,0,2,1:T(4,128)(2,1)S(1)}, u32[]{:S(2)}, u32[]{:S(2)}) async-start(bf16[4,32,5,2048]{3,0,2,1:T(4,128)(2,1)} %bitcast.48), calls=%async_computation.1 | async-start | bytes 5242880 | tf_op jit(solution)/shard_map/all_to_all | solution.py:92
  85.2 195.3 %reduce-scatter.8.cloned.1.call-start = ((), (), s32[]{:S(2)}) async-start(), calls=%async_computation.9 | async-start | bytes 7864320 | tf_op jit(solution)/shard_map/reduce_scatter | solution.py:39
  89.8 5.9 %copy-start.8 = (f32[64,8]{0,1:T(8,128)S(1)}, f32[64,8]{0,1:T(8,128)}, u32[]{:S(2)}) copy-start(f32[64,8]{0,1:T(8,128)} %param.9) | copy-start | bytes 6148
  182.9 1.6 copy-start.5
  192.1 129.4 %reduce-scatter.6.cloned.1.call-start = ((), (), s32[]{:S(2)}) async-start(), calls=%async_computation.8 | async-start | bytes 7864320 | tf_op jit(solution)/shard_map/reduce_scatter | solution.py:36
  192.1 8.7 %copy-start.4 = (bf16[4,32,5,2048]{3,0,2,1:T(4,128)(2,1)S(1)}, bf16[4,32,5,2048]{3,0,2,1:T(4,128)(2,1)}, u32[]{:S(2)}) copy-start(bf16[4,32,5,2048]{3,0,2,1:T(4,128)(2,1)} %copy-done.3) | copy-start | bytes 7864324
  200.0 0.8 copy-start.6
  208.4 179.9 %reduce-scatter.4.cloned.1.call-start = ((), (), s32[]{:S(2)}) async-start(), calls=%async_computation.7 | async-start | bytes 7864320 | tf_op jit(solution)/shard_map/reduce_scatter | solution.py:33
  216.2 5.2 %slice-start.4 = ((s8[6291456]{0:T(1024)(128)(4,1)}), s8[2097152]{0:T(1024)(128)(4,1)S(1)}, s32[]{:S(2)}) async-start(s8[6291456]{0:T(1024)(128)(4,1)} %bitcast.54), calls=%async_computation.14 | async-start | bytes 4194304
  216.2 5.2 %slice-start.5 = ((s8[6291456]{0:T(1024)(128)(4,1)}), s8[4194304]{0:T(1024)(128)(4,1)S(1)}, s32[]{:S(2)}) async-start(s8[6291456]{0:T(1024)(128)(4,1)} %bitcast.54), calls=%async_computation.15 | async-start | bytes 8388608
  216.2 5.2 %copy-start.7 = (bf16[4,160,384]{2,1,0:T(8,128)(2,1)S(1)}, bf16[4,160,384]{2,1,0:T(8,128)(2,1)}, u32[]{:S(2)}) copy-start(bf16[4,160,384]{2,1,0:T(8,128)(2,1)} %copy-done.6) | copy-start | bytes 1474564
  227.2 38.5 %all-to-all-start.3 = ((bf16[4,32,5,2048]{3,0,2,1:T(4,128)(2,1)}), bf16[4,32,5,2048]{3,0,2,1:T(4,128)(2,1)S(1)}, u32[]{:S(2)}, u32[]{:S(2)}) async-start(bf16[4,32,5,2048]{3,0,2,1:T(4,128)(2,1)} %bitcast.49), calls=%async_computation.3 | async-start | bytes 5242880 | tf_op jit(solution)/shard_map/all_to_all | solution.py:95
  273.5 114.8 %copy-start.1 = (bf16[64,2048]{1,0:T(8,128)(2,1)S(1)}, bf16[64,2048]{1,0:T(8,128)(2,1)}, u32[]{:S(2)}) copy-start(bf16[64,2048]{1,0:T(8,128)(2,1)} %param.10) | copy-start | bytes 786436
Sparse Core Ops, SparseCore 0:
  192.2 62.5 reduce-scatter.7
  257.8 63.6 reduce-scatter.5
  324.5 63.6 reduce-scatter.3
where the time goes:
time: 402 us; the launch traced here: 395 us
  waiting for transfers between devices  158 us (39%)
  blocking collectives  80.8 us (20%)
  local copies, waits for them, and re-layouts  62.3 us (15%)
  matrix products  51.6 us (13%)
  other arithmetic  15.9 us (4%)
  between operations  14.6 us (4%)
  starting transfers between devices  11.8 us (3%)
    reduce_scatter x1, waiting for transfers between devices, expert_backward(): lax.psum_scatter(grad_gate.astype(jnp.bfloat16), 'dp', scatter_dimension=...  66.7 us
    all_to_all x1, blocking collectives, shards(): lax.all_to_all(send_inputs, 'expert', split_axis=1, concat_axis=1, tiled=...  41.7 us
    reduce_scatter x1, waiting for transfers between devices, expert_backward(): lax.psum_scatter(grad_up.astype(jnp.bfloat16), 'dp', scatter_dimension=1,...  41 us
    all_to_all x1, blocking collectives, shards(): lax.all_to_all(send_upstream, 'expert', split_axis=1, concat_axis=1, tile...  39.2 us
    all_to_all x1, waiting for transfers between devices, shards(): lax.all_to_all(d_input.reshape(buffer_shape), 'expert', split_axis=1, con...  28 us
    all_to_all x1, waiting for transfers between devices, shards(): lax.all_to_all(output.reshape(buffer_shape), 'expert', split_axis=1, conc...  22.4 us
  transfers between devices with their start and end apart: 5, of which 4 were waited for; matrix products, arithmetic and copies ran while one was open for 16% of the time, Pallas kernels for 0%

commit v1 on v0

v1 whole, which is shorter than its diff:
```python
import functools

import jax
import jax.numpy as jnp
import numpy as np
from jax import lax
from jax.experimental import pallas as pl
from jax.experimental.pallas import tpu as pltpu
from jax.sharding import PartitionSpec as P

MESH = pl.DeviceIdType.MESH
CAP = 5
BF = jnp.bfloat16
F32 = jnp.float32
NT = (((1,), (1,)), ((), ()))
TN = (((0,), (0,)), ((), ()))


def mm(a, b, dims=None, precision=None):
    dims = (((1,), (0,)), ((), ())) if dims is None else dims
    return lax.dot_general(a, b, dims, preferred_element_type=F32, precision=precision)


def layer_kernel(
    n_e, n_dp,
    tok_ref, cot_ref, routes_ref, probs_ref, col_ref, row_ref, perm_ref, wg_hbm, wu_hbm, wd_hbm,
    mixed_ref, tgrad_ref, pgrad_ref, gg_hbm, gu_hbm, gd_hbm,
    sa, sb, ra, rb, ro, rd, x, u, q, g, gt, whi, wlo, wg, wu, wd, h, xs, us, pre_g, pre_u,
    w_sem, loc_sem, out_sem, snd, rcv, ysnd_r, yrcv_r, ysnd_h, yrcv_h,
):
    me = lax.axis_index("expert")
    my = lax.axis_index("dp")
    el = wg.shape[0]
    width = tok_ref.shape[1]
    chunk = width // n_dp
    t_n = tok_ref.shape[0]
    top = routes_ref.shape[1]
    n_x = n_e * el
    blocks = n_dp * el
    msg = blocks * CAP
    groups = n_e // blocks
    grows = blocks * msg
    per = blocks * CAP
    gd = 4
    gb = gd * msg

    w_copies = [
        pltpu.make_async_copy(src, dst, w_sem.at[i])
        for i, (src, dst) in enumerate(((wg_hbm, wg), (wu_hbm, wu), (wd_hbm, wd)))
    ]
    for copy in w_copies:
        copy.start()

    barrier = pltpu.get_barrier_semaphore()

    @pl.loop(1, n_e)
    def _(d):
        pl.semaphore_signal(barrier, inc=1, device_id={"expert": lax.rem(me + d, n_e)}, device_id_type=MESH)

    for d in range(1, n_dp):
        pl.semaphore_signal(barrier, inc=1, device_id={"dp": lax.rem(my + d, n_dp)}, device_id_type=MESH)

    routes = routes_ref[...]
    probs = probs_ref[...]
    totals = jnp.sum(probs, axis=1, keepdims=True)
    share = probs / totals
    lane_x = lax.broadcasted_iota(jnp.int32, (t_n, n_x), 1)
    named = jnp.zeros((t_n, n_x), F32)
    share_x = jnp.zeros((t_n, n_x), F32)
    for j in range(top):
        hit = routes[:, j : j + 1] == lane_x
        named = named + jnp.where(hit, 1.0, 0.0)
        share_x = share_x + jnp.where(hit, share[:, j : j + 1], 0.0)
    before = jnp.where(
        lax.broadcasted_iota(jnp.int32, (t_n, t_n), 0) > lax.broadcasted_iota(jnp.int32, (t_n, t_n), 1), 1.0, 0.0
    ).astype(BF)
    rank = mm(before, named.astype(BF))
    place = jnp.where(named > 0.0, rank, -1.0).astype(BF)
    place_c = jnp.concatenate([place] * n_dp, axis=0)
    share_c = jnp.concatenate([share_x] * n_dp, axis=0)
    tok_c = jnp.concatenate([tok_ref[:, c * chunk : (c + 1) * chunk] for c in range(n_dp)], axis=0)
    cot_c = jnp.concatenate([cot_ref[:, c * chunk : (c + 1) * chunk] for c in range(n_dp)], axis=0)

    pl.semaphore_wait(barrier, n_e - 1 + n_dp - 1)

    lane_e = lax.broadcasted_iota(jnp.int32, (gb, n_x), 1)
    lane_c = lax.broadcasted_iota(jnp.int32, (gb, n_dp * t_n), 1) // t_n
    col_e = col_ref[:, 0:1]
    col_s = col_ref[:, 1:2].astype(F32)
    col_c = col_ref[:, 2:3]
    n_g = n_e // gd

    def message(buf, i):
        return buf.at[pl.ds(pl.multiple_of(i * msg, msg), msg)]

    def send(kind, src, dst, o):
        @pl.when(o != me)
        def _():
            pltpu.make_async_remote_copy(
                src_ref=message(src, o), dst_ref=message(dst, me),
                send_sem=snd.at[kind, o], recv_sem=rcv.at[kind, me],
                device_id={"expert": o}, device_id_type=MESH,
            ).start()

        @pl.when(o == me)
        def _():
            pltpu.make_async_copy(message(src, o), message(dst, o), loc_sem.at[kind]).start()

    def await_from(kind, dst, i):
        @pl.when(i != me)
        def _():
            pltpu.make_async_remote_copy(
                src_ref=message(dst, i), dst_ref=message(dst, i),
                send_sem=snd.at[kind, i], recv_sem=rcv.at[kind, i],
                device_id={"expert": i}, device_id_type=MESH,
            ).wait_recv()

        @pl.when(i == me)
        def _():
            pltpu.make_async_copy(message(dst, i), message(dst, i), loc_sem.at[kind]).wait()

    def await_sent(kind, src):
        @pl.loop(0, n_e)
        def _(o):
            @pl.when(o != me)
            def _():
                pltpu.make_async_remote_copy(
                    src_ref=message(src, o), dst_ref=message(src, o),
                    send_sem=snd.at[kind, o], recv_sem=rcv.at[kind, o],
                    device_id={"expert": o}, device_id_type=MESH,
                ).wait_send()

    def await_group(kind, dst, gr):
        @pl.loop(0, blocks)
        def _(i):
            await_from(kind, dst, gr * blocks + i)

    def pick(og):
        return jnp.where(lane_e == col_e + og * (gd * el), 1.0, 0.0)

    @pl.loop(0, n_g)
    def _(i):
        og = lax.rem(me // gd + i, n_g)
        rows = pl.ds(pl.multiple_of(og * gb, gb), gb)
        held = mm(pick(og).astype(BF), place_c, NT)
        chosen = jnp.where((held == col_s) & (lane_c == col_c), 1.0, 0.0).astype(BF)
        g[rows, :] = chosen
        sa[rows, :] = mm(chosen, tok_c).astype(BF)
        for k in range(gd):
            send(0, sa, ra, og * gd + k)

    @pl.loop(0, n_g)
    def _(i):
        og = lax.rem(me // gd + i, n_g)
        rows = pl.ds(pl.multiple_of(og * gb, gb), gb)
        chosen = g[rows, :]
        scale = mm(pick(og), share_c, NT, lax.Precision.HIGHEST)
        scale = jnp.sum(scale * chosen.astype(F32), axis=1, keepdims=True)
        sb[rows, :] = (mm(chosen, cot_c) * scale).astype(BF)
        for k in range(gd):
            send(1, sb, rb, og * gd + k)

    half = grows // 2
    for p in range(2):
        q[p * half : (p + 1) * half, :] = jnp.where(
            lax.broadcasted_iota(jnp.int32, (half, grows), 1) == perm_ref[p * half : (p + 1) * half, 0:1], 1.0, 0.0
        ).astype(BF)
    tcols = n_e * msg // 4
    sub_e = lax.broadcasted_iota(jnp.int32, (n_x, tcols), 0)
    sub_c = lax.broadcasted_iota(jnp.int32, (n_dp * t_n, tcols), 0) // t_n
    for p in range(4):
        cols = slice(p * tcols, (p + 1) * tcols)
        pick_t = jnp.where(sub_e == row_ref[0:1, cols], 1.0, 0.0)
        held = mm(place_c, pick_t.astype(BF))
        here = (held == row_ref[1:2, cols].astype(F32)) & (sub_c == row_ref[2:3, cols])
        gt[:, cols] = jnp.where(here, 1.0, 0.0).astype(BF)
        weight = jnp.where(here, mm(share_c, pick_t, None, lax.Precision.HIGHEST), 0.0)
        high = weight.astype(BF)
        whi[:, cols] = high
        wlo[:, cols] = (weight - high.astype(F32)).astype(BF)

    def regroup(dst_write, src, gr):
        for p in range(2):
            dst_write(p, mm(q[p * half : (p + 1) * half, :], src[gr * grows : (gr + 1) * grows, :]).astype(BF))

    ex_rows = el * per

    def y_rows(kind, src, dst, gr):
        for d in range(1, n_dp):
            to = lax.rem(my + d, n_dp)
            pltpu.make_async_remote_copy(
                src_ref=src.at[gr, to], dst_ref=dst.at[my, gr],
                send_sem=ysnd_r.at[kind, gr, d], recv_sem=yrcv_r.at[kind, gr, my],
                device_id={"dp": to}, device_id_type=MESH,
            ).start()
        pltpu.make_async_copy(src.at[gr, my], dst.at[my, gr], yrcv_r.at[kind, gr, my]).start()

    def y_rows_wait(kind, src, dst, gr):
        for d in range(1, n_dp):
            frm = lax.rem(my + d, n_dp)
            pltpu.make_async_remote_copy(
                src_ref=src.at[gr, frm], dst_ref=dst.at[frm, gr],
                send_sem=ysnd_r.at[kind, gr, d], recv_sem=yrcv_r.at[kind, gr, frm],
                device_id={"dp": frm}, device_id_type=MESH,
            ).wait_recv()
        pltpu.make_async_copy(src.at[gr, my], dst.at[my, gr], yrcv_r.at[kind, gr, my]).wait()

    def y_hidden(kind, wait):
        for d in range(1, n_dp):
            to = lax.rem(my + d, n_dp)
            if wait:
                pltpu.make_async_remote_copy(
                    src_ref=h.at[kind, to], dst_ref=h.at[kind, to],
                    send_sem=ysnd_h.at[kind, d], recv_sem=yrcv_h.at[kind, to],
                    device_id={"dp": to}, device_id_type=MESH,
                ).wait_recv()
            else:
                pltpu.make_async_remote_copy(
                    src_ref=h.at[kind, my], dst_ref=h.at[kind, my],
                    send_sem=ysnd_h.at[kind, d], recv_sem=yrcv_h.at[kind, my],
                    device_id={"dp": to}, device_id_type=MESH,
                ).start()

    def into(dst, gr):
        def write(p, value):
            for c in range(n_dp // 2):
                dst[gr, p * (n_dp // 2) + c] = value[c * ex_rows : (c + 1) * ex_rows]
        return write

    for gr in range(groups):
        await_group(0, ra, gr)
        regroup(into(x, gr), ra, gr)
        y_rows(0, x, xs, gr)

    def rows_of(src, c, e):
        return jnp.concatenate([src[gr, c, pl.ds(pl.multiple_of(e * per, per), per), :] for gr in range(groups)], axis=0)

    def keep_hidden(kind, e, value):
        for gr in range(groups):
            h[kind, my, gr, pl.ds(pl.multiple_of(e * per, per), per), :] = value[gr * per : (gr + 1) * per]

    def keep_rows(dst, c, e, value):
        for gr in range(groups):
            dst[pl.ds(pl.multiple_of(gr * grows + (c * el + e) * per, per), per), :] = value[gr * per : (gr + 1) * per]

    w_copies[0].wait()
    w_copies[1].wait()
    w_copies[2].wait()

    @pl.loop(0, el)
    def _(e):
        gate = 0.0
        up = 0.0
        for c in range(n_dp):
            rows = rows_of(x, c, e)
            gate = gate + mm(rows, wg[e, c * chunk : (c + 1) * chunk, :])
            up = up + mm(rows, wu[e, c * chunk : (c + 1) * chunk, :])
        pre_g[e] = gate
        pre_u[e] = up
        active = (gate * jax.nn.sigmoid(gate) * up).astype(BF)
        keep_hidden(0, e, active)
        for c in range(n_dp):
            keep_rows(ra, c, e, mm(active, wd[e, c * chunk : (c + 1) * chunk, :], NT).astype(BF))

    y_hidden(0, False)
    await_sent(0, sa)

    def plain(dst, gr):
        def write(p, value):
            dst[gr * grows + p * half : gr * grows + (p + 1) * half, :] = value
        return write

    def send_group(kind, src, dst, gr):
        @pl.loop(0, blocks)
        def _(i):
            send(kind, src, dst, gr * blocks + lax.rem(me + i, blocks))

    for gr in range(groups):
        regroup(plain(sa, gr), ra, gr)
        send_group(2, sa, ro, gr)

    for gr in range(groups):
        await_group(1, rb, gr)
        regroup(into(u, gr), rb, gr)
        y_rows(1, u, us, gr)

    @pl.loop(0, el)
    def _(e):
        d_active = 0.0
        for c in range(n_dp):
            d_active = d_active + mm(rows_of(u, c, e), wd[e, c * chunk : (c + 1) * chunk, :])
        gate = pre_g[e]
        up = pre_u[e]
        sig = jax.nn.sigmoid(gate)
        d_gate = (d_active * up * sig * (1.0 + gate * (1.0 - sig))).astype(BF)
        d_up = (d_active * gate * sig).astype(BF)
        keep_hidden(1, e, d_gate)
        keep_hidden(2, e, d_up)
        for c in range(n_dp):
            cols = slice(c * chunk, (c + 1) * chunk)
            keep_rows(rb, c, e, (mm(d_gate, wg[e, cols, :], NT) + mm(d_up, wu[e, cols, :], NT)).astype(BF))

    y_hidden(1, False)
    y_hidden(2, False)
    await_sent(1, sb)
    for gr in range(groups):
        regroup(plain(sb, gr), rb, gr)
        send_group(3, sb, rd, gr)

    for gr in range(groups):
        await_group(2, ro, gr)
    mixed = mm(whi[...], ro[...]) + mm(wlo[...], ro[...])
    for c in range(n_dp):
        mixed_ref[:, c * chunk : (c + 1) * chunk] = mixed[c * t_n : (c + 1) * t_n].astype(BF)
    grad_x = jnp.zeros((n_dp * t_n, n_x), F32)
    for og in range(n_g):
        rows = slice(og * gb, (og + 1) * gb)
        dots = jnp.sum(mm(g[rows, :], cot_c) * ro[rows, :].astype(F32), axis=1, keepdims=True)
        spread = pick(og) * dots
        high = spread.astype(BF)
        low = (spread - high.astype(F32)).astype(BF)
        grad_x = grad_x + mm(gt[:, rows], high) + mm(gt[:, rows], low)
    share_grad_x = grad_x[0:t_n]
    for c in range(1, n_dp):
        share_grad_x = share_grad_x + grad_x[c * t_n : (c + 1) * t_n]
    inner = jnp.sum(share_grad_x * share_x, axis=1, keepdims=True)
    for j in range(top):
        mine = jnp.sum(jnp.where(routes[:, j : j + 1] == lane_x, share_grad_x, 0.0), axis=1, keepdims=True)
        pgrad_ref[:, j : j + 1] = (mine - inner) / totals

    def gathered(src, e):
        return jnp.concatenate(
            [src[r, gr, pl.ds(pl.multiple_of(e * per, per), per), :] for r in range(n_dp) for gr in range(groups)], axis=0
        )

    def hidden_of(kind, e):
        return jnp.concatenate(
            [h[kind, r, gr, pl.ds(pl.multiple_of(e * per, per), per), :] for r in range(n_dp) for gr in range(groups)],
            axis=0,
        )

    y_hidden(0, True)
    for gr in range(groups):
        y_rows_wait(1, u, us, gr)

    @pl.loop(0, el)
    def _(e):
        wg[e, 2 * chunk : 3 * chunk, :] = mm(gathered(us, e), hidden_of(0, e), TN).astype(BF)

    out_d = pltpu.make_async_copy(wg.at[:, 2 * chunk : 3 * chunk], gd_hbm, out_sem.at[2])
    out_d.start()

    for gr in range(groups):
        y_rows_wait(0, x, xs, gr)
    y_hidden(1, True)

    @pl.loop(0, el)
    def _(e):
        wg[e, 0 * chunk : 1 * chunk, :] = mm(gathered(xs, e), hidden_of(1, e), TN).astype(BF)

    out_g = pltpu.make_async_copy(wg.at[:, 0 * chunk : 1 * chunk], gg_hbm, out_sem.at[0])
    out_g.start()
    y_hidden(2, True)

    @pl.loop(0, el)
    def _(e):
        wg[e, 1 * chunk : 2 * chunk, :] = mm(gathered(xs, e), hidden_of(2, e), TN).astype(BF)

    out_u = pltpu.make_async_copy(wg.at[:, 1 * chunk : 2 * chunk], gu_hbm, out_sem.at[1])
    out_u.start()

    for gr in range(groups):
        await_group(3, rd, gr)
    tgrad = mm(gt[...], rd[...])
    for c in range(n_dp):
        tgrad_ref[:, c * chunk : (c + 1) * chunk] = tgrad[c * t_n : (c + 1) * t_n].astype(BF)

    await_sent(2, sa)
    await_sent(3, sb)
    for d in range(1, n_dp):
        to = lax.rem(my + d, n_dp)
        for kind, (src, dst) in enumerate(((x, xs), (u, us))):
            for gr in range(groups):
                pltpu.make_async_remote_copy(
                    src_ref=src.at[gr, to], dst_ref=dst.at[my, gr],
                    send_sem=ysnd_r.at[kind, gr, d], recv_sem=yrcv_r.at[kind, gr, my],
                    device_id={"dp": to}, device_id_type=MESH,
                ).wait_send()
        for kind in range(3):
            pltpu.make_async_remote_copy(
                src_ref=h.at[kind, my], dst_ref=h.at[kind, my],
                send_sem=ysnd_h.at[kind, d], recv_sem=yrcv_h.at[kind, my],
                device_id={"dp": to}, device_id_type=MESH,
            ).wait_send()
    out_d.wait()
    out_g.wait()
    out_u.wait()


def shards(n_e, n_dp, tokens, routes, probs, cotangent, w_gate, w_up, w_down):
    t_n, width = tokens.shape
    el, _, hid = w_gate.shape
    chunk = width // n_dp
    blocks = n_dp * el
    msg = blocks * CAP
    groups = n_e // blocks
    grows = blocks * msg
    slots = n_e * msg
    gb = 4 * msg
    i = np.arange(slots)
    m = i % msg
    local, seat, part = (m % (el * CAP)) // CAP, i % CAP, m // (el * CAP)
    col = np.zeros((gb, 4), np.int32)
    col[:, 0] = ((i // msg) * el + local)[:gb]
    col[:, 1], col[:, 2] = seat[:gb], part[:gb]
    row = np.zeros((8, slots), np.int32)
    row[0], row[1], row[2] = (i // msg) * el + local, seat, part
    j = np.arange(grows)
    perm = (((j % msg) // CAP) * msg + (j // msg) * CAP + j % CAP).astype(np.int32)[:, None]
    vmem = pl.BlockSpec(memory_space=pltpu.VMEM)
    hbm = pl.BlockSpec(memory_space=pl.ANY)
    dma = pltpu.SemaphoreType.DMA
    grad = jax.ShapeDtypeStruct((el, chunk, hid), BF)
    V = pltpu.VMEM
    return pl.pallas_call(
        functools.partial(layer_kernel, n_e, n_dp),
        out_shape=(
            jax.ShapeDtypeStruct((t_n, width), BF),
            jax.ShapeDtypeStruct((t_n, width), BF),
            jax.ShapeDtypeStruct(probs.shape, F32),
            grad, grad, grad,
        ),
        in_specs=[vmem] * 7 + [hbm] * 3,
        out_specs=[vmem] * 3 + [hbm] * 3,
        scratch_shapes=[V((slots, chunk), BF)] * 6
        + [V((groups, n_dp, el * msg, chunk), BF)] * 2
        + [V((grows, grows), BF), V((slots, n_dp * t_n), BF)]
        + [V((n_dp * t_n, slots), BF)] * 3
        + [V(w_gate.shape, BF)] * 3
        + [V((3, n_dp, groups, el * msg, hid), BF)]
        + [V((n_dp, groups, el * msg, chunk), BF)] * 2
        + [V((el, groups * msg, hid), F32)] * 2
        + [dma((3,)), dma((4,)), dma((3,)), dma((4, n_e)), dma((4, n_e)),
           dma((2, groups, n_dp)), dma((2, groups, n_dp)), dma((3, n_dp)), dma((3, n_dp))],
        compiler_params=pltpu.CompilerParams(collective_id=0, has_side_effects=True, vmem_limit_bytes=67043328),
    )(tokens, cotangent, routes, probs, jnp.asarray(col), jnp.asarray(row), jnp.asarray(perm), w_gate, w_up, w_down)


def solution(mesh):
    both = P(("expert", "dp"), None)
    return jax.shard_map(
        functools.partial(shards, mesh.shape["expert"], mesh.shape["dp"]),
        mesh=mesh,
        in_specs=(both, both, both, both) + (P("expert", None, None),) * 3,
        out_specs=(both, both, both) + (P("expert", "dp", None),) * 3,
        check_vma=False,
    )
```

time: 402 us -> 195 us (0.49); the launches traced: 395 us -> 192 us
  Pallas kernels: 0 us -> 178 us
  waiting for transfers between devices: 158 us -> 0 us
  blocking collectives: 80.8 us -> 0 us
  matrix products: 51.6 us -> 0 us
  local copies, waits for them, and re-layouts: 62.3 us -> 13.5 us
  other arithmetic: 15.9 us -> 0 us
  between operations: 14.6 us -> 0.65 us
  starting transfers between devices: 11.8 us -> 0 us
    pallas_call x0 -> x1, Pallas kernels: none -> 178 us  [shards(): pl.pallas_call(functools.partial(layer_kernel, n_e, n_dp), out_shape=(jax...]
    reduce_scatter x3 -> x0, waiting for transfers between devices: 108 us -> none  [the longest x1 66.7 us: expert_backward(): lax.psum_scatter(grad_gate.astype(jnp.bfloat16), 'dp', scatter_dimension=...]
    all_to_all x2 -> x0, blocking collectives: 80.8 us -> none  [the longest x1 41.7 us: shards(): lax.all_to_all(send_inputs, 'expert', split_axis=1, concat_axis=1, tiled=...]
    dot_general x10 -> x0, matrix products: 51.6 us -> none  [the longest x1 7.89 us: expert_backward(): jnp.einsum('krd,kdh->krh', upstream, w_down, preferred_element_type=jnp.f...]
    all_to_all x2 -> x0, waiting for transfers between devices: 50.5 us -> none  [the longest x1 28 us: shards(): lax.all_to_all(d_input.reshape(buffer_shape), 'expert', split_axis=1, con...]
    gather x6 -> x0, local copies, waits for them, and re-layouts: 21.3 us -> none  [the longest x2 6.28 us: shards(): tokens[token_index]]
    convert_element_type x3 -> x0, local copies, waits for them, and re-layouts: 13 us -> none  [the longest x1 5.94 us: shards(): cotangent[token_index].astype(jnp.float32)]
    all_to_all x2 -> x0, starting transfers between devices: 11 us -> none  [the longest x1 5.69 us: shards(): lax.all_to_all(d_input.reshape(buffer_shape), 'expert', split_axis=1, con...]
  transfers between devices with their start and end apart: 5 -> 0, of which waited for: 4 -> 0; matrix products, arithmetic and copies ran while one was open for 16% -> 0% of each run, Pallas kernels for 0% -> 0%
where the time goes in v1:
time: 195 us; the launch traced here: 192 us
  Pallas kernels  178 us (91%)
  local copies, waits for them, and re-layouts  13.5 us (7%)
    pallas_call x1, Pallas kernels, shards(): pl.pallas_call(functools.partial(layer_kernel, n_e, n_dp), out_shape=(jax...  178 us
    unnamed x11, local copies, waits for them, and re-layouts  12.1 us

profile of v1, /device:TPU:7, one launch (start us, length us, event | category | flops | bytes accessed | tf_op | source)
XLA Modules:
  0.0 192.3 jit_solution(3748346509442741891)
XLA Ops:
  0.6 1.4 copy.16.routes_ref
  2.0 1.4 copy.17.probs_ref
  3.4 178.1 %shard_map.145 = (bf16[64,2048]{1,0:T(8,128)(2,1)}, bf16[64,2048]{1,0:T(8,128)(2,1)}, f32[64,8]{1,0:T(8,128)}, bf16[4,512,384]{2,1,0:T(8,128)(2,1)}, bf16[4,512,...) custom-call(bf16[64,2048]{1,0:T(8,128)(2,1)} %tok_ref.1, bf16[64,2048]{1,0:T(8,128)(2,1)} %cot_ref.1, ...), custom_call_target="tpu_custom_call" | custom-call | tf_op jit(solution)/shard_map/pallas_call | solution.py:425
  181.5 1.4 copy.18
  183.0 1.7 copy.24
  184.6 1.7 copy.25
  186.3 0.0 copy-start.1
  186.3 2.8 %copy.26 = bf16[4,512,384]{2,1,0:T(8,128)(2,1)} copy(bf16[4,512,384]{2,1,0:T(8,128)(2,1)} %get-tuple-element.21) | data formatting | bytes 3145728
  189.1 0.0 copy-done.1
  189.1 0.0 copy-start
  189.1 1.1 copy.27
  190.3 0.8 copy-done
  191.1 1.1 copy.28
Async XLA Ops:
  186.3 2.8 %copy-start.1 = (bf16[4,512,384]{2,1,0:T(8,128)(2,1)S(1)}, bf16[4,512,384]{2,1,0:T(8,128)(2,1)}, u32[]{:S(2)}) copy-start(bf16[4,512,384]{2,1,0:T(8,128)(2,1)} %get-tuple-element.22) | copy-start | bytes 4718596
  189.1 2.0 %copy-start = (bf16[4,512,384]{2,1,0:T(8,128)(2,1)S(1)}, bf16[4,512,384]{2,1,0:T(8,128)(2,1)}, u32[]{:S(2)}) copy-start(bf16[4,512,384]{2,1,0:T(8,128)(2,1)} %get-tuple-element.23) | copy-start | bytes 4718596

commit v2 on v1

--- a/solution.py
+++ b/solution.py
@@ -26,7 +26,7 @@
     tok_ref, cot_ref, routes_ref, probs_ref, col_ref, row_ref, perm_ref, wg_hbm, wu_hbm, wd_hbm,
     mixed_ref, tgrad_ref, pgrad_ref, gg_hbm, gu_hbm, gd_hbm,
     sa, sb, ra, rb, ro, rd, x, u, q, g, gt, whi, wlo, wg, wu, wd, h, xs, us, pre_g, pre_u,
-    w_sem, loc_sem, out_sem, snd, rcv, ysnd_r, yrcv_r, ysnd_h, yrcv_h,
+    w_sem, loc_sem, out_sem, snd, rcv, ysnd_r, yrcv_r, ysnd_h, yrcv_h, ysnd_f, yrcv_f,
 ):
     me = lax.axis_index("expert")
     my = lax.axis_index("dp")
@@ -34,7 +34,7 @@
     width = tok_ref.shape[1]
     chunk = width // n_dp
     t_n = tok_ref.shape[0]
-    top = routes_ref.shape[1]
+    top = routes_ref.shape[0]
     n_x = n_e * el
     blocks = n_dp * el
     msg = blocks * CAP
@@ -60,15 +60,22 @@
     for d in range(1, n_dp):
         pl.semaphore_signal(barrier, inc=1, device_id={"dp": lax.rem(my + d, n_dp)}, device_id_type=MESH)
 
-    routes = routes_ref[...]
-    probs = probs_ref[...]
+    def eye(n):
+        return jnp.where(
+            lax.broadcasted_iota(jnp.int32, (n, n), 0) == lax.broadcasted_iota(jnp.int32, (n, n), 1), 1.0, 0.0
+        )
+
+    exact = lax.Precision.HIGHEST
+    routes = mm(routes_ref[...].astype(F32), eye(top), TN, exact)
+    probs = mm(probs_ref[...], eye(top), TN, exact)
     totals = jnp.sum(probs, axis=1, keepdims=True)
     share = probs / totals
     lane_x = lax.broadcasted_iota(jnp.int32, (t_n, n_x), 1)
+    lane_f = lane_x.astype(F32)
     named = jnp.zeros((t_n, n_x), F32)
     share_x = jnp.zeros((t_n, n_x), F32)
     for j in range(top):
-        hit = routes[:, j : j + 1] == lane_x
+        hit = routes[:, j : j + 1] == lane_f
         named = named + jnp.where(hit, 1.0, 0.0)
         share_x = share_x + jnp.where(hit, share[:, j : j + 1], 0.0)
     before = jnp.where(
@@ -90,75 +97,92 @@
     col_c = col_ref[:, 2:3]
     n_g = n_e // gd
 
-    def message(buf, i):
-        return buf.at[pl.ds(pl.multiple_of(i * msg, msg), msg)]
-
-    def send(kind, src, dst, o):
+    halves = 2
+    hw = chunk // halves
+
+    def message(buf, i, hf=None):
+        rows = pl.ds(pl.multiple_of(i * msg, msg), msg)
+        return buf.at[rows] if hf is None else buf.at[rows, pl.ds(hf * hw, hw)]
+
+    def send(kind, src, dst, o, hf):
         @pl.when(o != me)
         def _():
             pltpu.make_async_remote_copy(
-                src_ref=message(src, o), dst_ref=message(dst, me),
-                send_sem=snd.at[kind, o], recv_sem=rcv.at[kind, me],
+                src_ref=message(src, o, hf), dst_ref=message(dst, me, hf),
+                send_sem=snd.at[kind, hf, o], recv_sem=rcv.at[kind, hf, me],
                 device_id={"expert": o}, device_id_type=MESH,
             ).start()
 
         @pl.when(o == me)
         def _():
-            pltpu.make_async_copy(message(src, o), message(dst, o), loc_sem.at[kind]).start()
-
-    def await_from(kind, dst, i):
+            pltpu.make_async_copy(message(src, o, hf), message(dst, o, hf), loc_sem.at[kind, hf]).start()
+
+    def send_all(kind, src, dst, hf):
+        @pl.loop(0, 8)
+        def _(i):
+            k = i // 2
+            z = lax.rem(me // 8 + 2 + 3 * k + 3 * (k // 2) + 2 * (k // 3), 4)
+            core = lax.rem(me + i, 2)
+            for dx in (2, 1, 3, 0):
+                send(kind, src, dst, z * 8 + lax.rem(me // 2 + dx, 4) * 2 + core, hf)
+
+    def await_from(kind, dst, i, hf):
         @pl.when(i != me)
         def _():
             pltpu.make_async_remote_copy(
-                src_ref=message(dst, i), dst_ref=message(dst, i),
-                send_sem=snd.at[kind, i], recv_sem=rcv.at[kind, i],
+                src_ref=message(dst, i, hf), dst_ref=message(dst, i, hf),
+                send_sem=snd.at[kind, hf, i], recv_sem=rcv.at[kind, hf, i],
                 device_id={"expert": i}, device_id_type=MESH,
             ).wait_recv()
 
         @pl.when(i == me)
         def _():
-            pltpu.make_async_copy(message(dst, i), message(dst, i), loc_sem.at[kind]).wait()
+            pltpu.make_async_copy(message(dst, i, hf), message(dst, i, hf), loc_sem.at[kind, hf]).wait()
 
     def await_sent(kind, src):
         @pl.loop(0, n_e)
         def _(o):
             @pl.when(o != me)
             def _():
-                pltpu.make_async_remote_copy(
-                    src_ref=message(src, o), dst_ref=message(src, o),
-                    send_sem=snd.at[kind, o], recv_sem=rcv.at[kind, o],
-                    device_id={"expert": o}, device_id_type=MESH,
-                ).wait_send()
-
-    def await_group(kind, dst, gr):
-        @pl.loop(0, blocks)
+                for hf in range(halves):
+                    pltpu.make_async_remote_copy(
+                        src_ref=message(src, o, hf), dst_ref=message(src, o, hf),
+                        send_sem=snd.at[kind, hf, o], recv_sem=rcv.at[kind, hf, o],
+                        device_id={"expert": o}, device_id_type=MESH,
+                    ).wait_send()
+
+    def await_all(kind, dst, hf):
+        @pl.loop(0, n_e)
         def _(i):
-            await_from(kind, dst, gr * blocks + i)
+            await_from(kind, dst, i, hf)
 
     def pick(og):
         return jnp.where(lane_e == col_e + og * (gd * el), 1.0, 0.0)
 
     @pl.loop(0, n_g)
     def _(i):
-        og = lax.rem(me // gd + i, n_g)
+        og = lax.rem(me // gd + 5 * i + 5, n_g)
         rows = pl.ds(pl.multiple_of(og * gb, gb), gb)
         held = mm(pick(og).astype(BF), place_c, NT)
         chosen = jnp.where((held == col_s) & (lane_c == col_c), 1.0, 0.0).astype(BF)
         g[rows, :] = chosen
         sa[rows, :] = mm(chosen, tok_c).astype(BF)
         for k in range(gd):
-            send(0, sa, ra, og * gd + k)
+            send(0, sa, ra, og * gd + k, 0)
+
+    send_all(0, sa, ra, 1)
 
     @pl.loop(0, n_g)
     def _(i):
-        og = lax.rem(me // gd + i, n_g)
+        og = lax.rem(me // gd + 5 * i + 5, n_g)
         rows = pl.ds(pl.multiple_of(og * gb, gb), gb)
         chosen = g[rows, :]
         scale = mm(pick(og), share_c, NT, lax.Precision.HIGHEST)
         scale = jnp.sum(scale * chosen.astype(F32), axis=1, keepdims=True)
         sb[rows, :] = (mm(chosen, cot_c) * scale).astype(BF)
-        for k in range(gd):
-            send(1, sb, rb, og * gd + k)
+
+    send_all(1, sb, rb, 0)
+    send_all(1, sb, rb, 1)
 
     half = grows // 2
     for p in range(2):
@@ -179,58 +203,84 @@
         whi[:, cols] = high
         wlo[:, cols] = (weight - high.astype(F32)).astype(BF)
 
-    def regroup(dst_write, src, gr):
+    def regroup(dst_write, src, gr, hf):
+        cols = slice(0, chunk) if hf is None else slice(hf * hw, (hf + 1) * hw)
         for p in range(2):
-            dst_write(p, mm(q[p * half : (p + 1) * half, :], src[gr * grows : (gr + 1) * grows, :]).astype(BF))
+            dst_write(p, mm(q[p * half : (p + 1) * half, :], src[gr * grows : (gr + 1) * grows, cols]).astype(BF))
 
     ex_rows = el * per
 
-    def y_rows(kind, src, dst, gr):
-        for d in range(1, n_dp):
+    def y_rows(kind, src, dst, gr, hf):
+        cols = pl.ds(hf * hw, hw)
+        for d in (1, n_dp - 1, 2):
             to = lax.rem(my + d, n_dp)
             pltpu.make_async_remote_copy(
-                src_ref=src.at[gr, to], dst_ref=dst.at[my, gr],
-                send_sem=ysnd_r.at[kind, gr, d], recv_sem=yrcv_r.at[kind, gr, my],
+                src_ref=src.at[gr, to, :, cols], dst_ref=dst.at[my, gr, :, cols],
+                send_sem=ysnd_r.at[kind, gr, hf, d], recv_sem=yrcv_r.at[kind, gr, hf, my],
                 device_id={"dp": to}, device_id_type=MESH,
             ).start()
-        pltpu.make_async_copy(src.at[gr, my], dst.at[my, gr], yrcv_r.at[kind, gr, my]).start()
-
-    def y_rows_wait(kind, src, dst, gr):
+        pltpu.make_async_copy(
+            src.at[gr, my, :, cols], dst.at[my, gr, :, cols], yrcv_r.at[kind, gr, hf, my]
+        ).start()
+
+    def y_rows_wait(kind, src, dst, gr, hf):
+        cols = pl.ds(hf * hw, hw)
         for d in range(1, n_dp):
             frm = lax.rem(my + d, n_dp)
             pltpu.make_async_remote_copy(
-                src_ref=src.at[gr, frm], dst_ref=dst.at[frm, gr],
-                send_sem=ysnd_r.at[kind, gr, d], recv_sem=yrcv_r.at[kind, gr, frm],
+                src_ref=src.at[gr, frm, :, cols], dst_ref=dst.at[frm, gr, :, cols],
+                send_sem=ysnd_r.at[kind, gr, hf, d], recv_sem=yrcv_r.at[kind, gr, hf, frm],
                 device_id={"dp": frm}, device_id_type=MESH,
             ).wait_recv()
-        pltpu.make_async_copy(src.at[gr, my], dst.at[my, gr], yrcv_r.at[kind, gr, my]).wait()
-
-    def y_hidden(kind, wait):
-        for d in range(1, n_dp):
-            to = lax.rem(my + d, n_dp)
-            if wait:
-                pltpu.make_async_remote_copy(
-                    src_ref=h.at[kind, to], dst_ref=h.at[kind, to],
-                    send_sem=ysnd_h.at[kind, d], recv_sem=yrcv_h.at[kind, to],
-                    device_id={"dp": to}, device_id_type=MESH,
-                ).wait_recv()
-            else:
-                pltpu.make_async_remote_copy(
-                    src_ref=h.at[kind, my], dst_ref=h.at[kind, my],
-                    send_sem=ysnd_h.at[kind, d], recv_sem=yrcv_h.at[kind, my],
-                    device_id={"dp": to}, device_id_type=MESH,
-                ).start()
-
-    def into(dst, gr):
+        pltpu.make_async_copy(
+            src.at[gr, my, :, cols], dst.at[my, gr, :, cols], yrcv_r.at[kind, gr, hf, my]
+        ).wait()
+
+    far = lax.rem(my + 2, n_dp)
+    sides = (lax.rem(my + 1, n_dp), lax.rem(my + n_dp - 1, n_dp))
+
+    def y_hidden(kind):
+        for i in range(2):
+            pltpu.make_async_remote_copy(
+                src_ref=h.at[kind, my], dst_ref=h.at[kind, my],
+                send_sem=ysnd_h.at[kind, i], recv_sem=yrcv_h.at[kind, i],
+                device_id={"dp": sides[i]}, device_id_type=MESH,
+            ).start()
+
+    def hand_on(kind, i):
+        held = sides[1 - i]
+        pltpu.make_async_remote_copy(
+            src_ref=h.at[kind, held], dst_ref=h.at[kind, held],
+            send_sem=ysnd_h.at[kind, i], recv_sem=yrcv_h.at[kind, i],
+            device_id={"dp": held}, device_id_type=MESH,
+        ).wait_recv()
+        pltpu.make_async_remote_copy(
+            src_ref=h.at[kind, held, i], dst_ref=h.at[kind, held, i],
+            send_sem=ysnd_f.at[kind, i], recv_sem=yrcv_f.at[kind, i],
+            device_id={"dp": sides[i]}, device_id_type=MESH,
+        ).start()
+
+    def y_hidden_far(kind):
+        for i in range(2):
+            pltpu.make_async_remote_copy(
+                src_ref=h.at[kind, far, i], dst_ref=h.at[kind, far, i],
+                send_sem=ysnd_f.at[kind, i], recv_sem=yrcv_f.at[kind, i],
+                device_id={"dp": sides[i]}, device_id_type=MESH,
+            ).wait_recv()
+
+    def into(dst, gr, hf):
+        cols = slice(hf * hw, (hf + 1) * hw)
+
         def write(p, value):
             for c in range(n_dp // 2):
-                dst[gr, p * (n_dp // 2) + c] = value[c * ex_rows : (c + 1) * ex_rows]
+                dst[gr, p * (n_dp // 2) + c, :, cols] = value[c * ex_rows : (c + 1) * ex_rows]
         return write
 
-    for gr in range(groups):
-        await_group(0, ra, gr)
-        regroup(into(x, gr), ra, gr)
-        y_rows(0, x, xs, gr)
+    for hf in range(halves):
+        await_all(0, ra, hf)
+        for gr in range(groups):
+            regroup(into(x, gr, hf), ra, gr, hf)
+            y_rows(0, x, xs, gr, hf)
 
     def rows_of(src, c, e):
         return jnp.concatenate([src[gr, c, pl.ds(pl.multiple_of(e * per, per), per), :] for gr in range(groups)], axis=0)
@@ -262,7 +312,7 @@
         for c in range(n_dp):
             keep_rows(ra, c, e, mm(active, wd[e, c * chunk : (c + 1) * chunk, :], NT).astype(BF))
 
-    y_hidden(0, False)
+    y_hidden(0)
     await_sent(0, sa)
 
     def plain(dst, gr):
@@ -270,19 +320,20 @@
             dst[gr * grows + p * half : gr * grows + (p + 1) * half, :] = value
         return write
 
-    def send_group(kind, src, dst, gr):
-        @pl.loop(0, blocks)
-        def _(i):
-            send(kind, src, dst, gr * blocks + lax.rem(me + i, blocks))
-
     for gr in range(groups):
-        regroup(plain(sa, gr), ra, gr)
-        send_group(2, sa, ro, gr)
-
-    for gr in range(groups):
-        await_group(1, rb, gr)
-        regroup(into(u, gr), rb, gr)
-        y_rows(1, u, us, gr)
+        regroup(plain(sa, gr), ra, gr, None)
+    for hf in range(halves):
+        send_all(2, sa, ro, hf)
+
+    for hf in range(halves):
+        await_all(1, rb, hf)
+        for gr in range(groups):
+            regroup(into(u, gr, hf), rb, gr, hf)
+        if hf == 0:
+            hand_on(0, 0)
+            hand_on(0, 1)
+        for gr in range(groups):
+            y_rows(1, u, us, gr, hf)
 
     @pl.loop(0, el)
     def _(e):
@@ -300,15 +351,16 @@
             cols = slice(c * chunk, (c + 1) * chunk)
             keep_rows(rb, c, e, (mm(d_gate, wg[e, cols, :], NT) + mm(d_up, wu[e, cols, :], NT)).astype(BF))
 
-    y_hidden(1, False)
-    y_hidden(2, False)
+    y_hidden(1)
+    y_hidden(2)
     await_sent(1, sb)
     for gr in range(groups):
-        regroup(plain(sb, gr), rb, gr)
-        send_group(3, sb, rd, gr)
-
-    for gr in range(groups):
-        await_group(2, ro, gr)
+        regroup(plain(sb, gr), rb, gr, None)
+    for hf in range(halves):
+        send_all(3, sb, rd, hf)
+
+    for hf in range(halves):
+        await_all(2, ro, hf)
     mixed = mm(whi[...], ro[...]) + mm(wlo[...], ro[...])
     for c in range(n_dp):
         mixed_ref[:, c * chunk : (c + 1) * chunk] = mixed[c * t_n : (c + 1) * t_n].astype(BF)
@@ -324,9 +376,15 @@
     for c in range(1, n_dp):
         share_grad_x = share_grad_x + grad_x[c * t_n : (c + 1) * t_n]
     inner = jnp.sum(share_grad_x * share_x, axis=1, keepdims=True)
+    grads = []
     for j in range(top):
-        mine = jnp.sum(jnp.where(routes[:, j : j + 1] == lane_x, share_grad_x, 0.0), axis=1, keepdims=True)
-        pgrad_ref[:, j : j + 1] = (mine - inner) / totals
+        mine = jnp.sum(jnp.where(routes[:, j : j + 1] == lane_f, share_grad_x, 0.0), axis=1, keepdims=True)
+        grads.append((mine - inner) / totals)
+    lane_j = lax.broadcasted_iota(jnp.int32, (t_n, top), 1)
+    prob_grad = jnp.zeros((t_n, top), F32)
+    for j in range(top):
+        prob_grad = jnp.where(lane_j == j, grads[j], prob_grad)
+    pgrad_ref[...] = mm(prob_grad, eye(t_n), TN, exact)
 
     def gathered(src, e):
         return jnp.concatenate(
@@ -339,9 +397,11 @@
             axis=0,
         )
 
-    y_hidden(0, True)
-    for gr in range(groups):
-        y_rows_wait(1, u, us, gr)
+    y_hidden_far(0)
+    for hf in range(halves):
+        for gr in range(groups):
+            y_rows_wait(1, u, us, gr, hf)
+            y_rows_wait(0, x, xs, gr, hf)
 
     @pl.loop(0, el)
     def _(e):
@@ -350,9 +410,17 @@
     out_d = pltpu.make_async_copy(wg.at[:, 2 * chunk : 3 * chunk], gd_hbm, out_sem.at[2])
     out_d.start()
 
-    for gr in range(groups):
-        y_rows_wait(0, x, xs, gr)
-    y_hidden(1, True)
+    for kind in (1, 2):
+        hand_on(kind, 0)
+        hand_on(kind, 1)
+
+    for hf in range(halves):
+        await_all(3, rd, hf)
+    tgrad = mm(gt[...], rd[...])
+    for c in range(n_dp):
+        tgrad_ref[:, c * chunk : (c + 1) * chunk] = tgrad[c * t_n : (c + 1) * t_n].astype(BF)
+
+    y_hidden_far(1)
 
     @pl.loop(0, el)
     def _(e):
@@ -360,7 +428,7 @@
 
     out_g = pltpu.make_async_copy(wg.at[:, 0 * chunk : 1 * chunk], gg_hbm, out_sem.at[0])
     out_g.start()
-    y_hidden(2, True)
+    y_hidden_far(2)
 
     @pl.loop(0, el)
     def _(e):
@@ -368,12 +436,6 @@
 
     out_u = pltpu.make_async_copy(wg.at[:, 1 * chunk : 2 * chunk], gu_hbm, out_sem.at[1])
     out_u.start()
-
-    for gr in range(groups):
-        await_group(3, rd, gr)
-    tgrad = mm(gt[...], rd[...])
-    for c in range(n_dp):
-        tgrad_ref[:, c * chunk : (c + 1) * chunk] = tgrad[c * t_n : (c + 1) * t_n].astype(BF)
 
     await_sent(2, sa)
     await_sent(3, sb)
@@ -381,20 +443,42 @@
         to = lax.rem(my + d, n_dp)
         for kind, (src, dst) in enumerate(((x, xs), (u, us))):
             for gr in range(groups):
-                pltpu.make_async_remote_copy(
-                    src_ref=src.at[gr, to], dst_ref=dst.at[my, gr],
-                    send_sem=ysnd_r.at[kind, gr, d], recv_sem=yrcv_r.at[kind, gr, my],
-                    device_id={"dp": to}, device_id_type=MESH,
-                ).wait_send()
-        for kind in range(3):
+                for hf in range(halves):
+                    cols = pl.ds(hf * hw, hw)
+                    pltpu.make_async_remote_copy(
+                        src_ref=src.at[gr, to, :, cols], dst_ref=dst.at[my, gr, :, cols],
+                        send_sem=ysnd_r.at[kind, gr, hf, d], recv_sem=yrcv_r.at[kind, gr, hf, my],
+                        device_id={"dp": to}, device_id_type=MESH,
+                    ).wait_send()
+    for kind in range(3):
+        for i in range(2):
             pltpu.make_async_remote_copy(
                 src_ref=h.at[kind, my], dst_ref=h.at[kind, my],
-                send_sem=ysnd_h.at[kind, d], recv_sem=yrcv_h.at[kind, my],
-                device_id={"dp": to}, device_id_type=MESH,
+                send_sem=ysnd_h.at[kind, i], recv_sem=yrcv_h.at[kind, i],
+                device_id={"dp": sides[i]}, device_id_type=MESH,
+            ).wait_send()
+            pltpu.make_async_remote_copy(
+                src_ref=h.at[kind, my, i], dst_ref=h.at[kind, my, i],
+                send_sem=ysnd_f.at[kind, i], recv_sem=yrcv_f.at[kind, i],
+                device_id={"dp": sides[i]}, device_id_type=MESH,
             ).wait_send()
     out_d.wait()
     out_g.wait()
     out_u.wait()
+
+
+def hand_out(*refs):
+    count = (len(refs) - 1) // 3
+    srcs, dsts, held, sem = refs[:count], refs[count : 2 * count], refs[2 * count : 3 * count], refs[-1]
+    inward = [pltpu.make_async_copy(srcs[i], held[i], sem.at[0, i]) for i in range(count)]
+    outward = [pltpu.make_async_copy(held[i], dsts[i], sem.at[1, i]) for i in range(count)]
+    for copy in inward:
+        copy.start()
+    for i in range(count):
+        inward[i].wait()
+        outward[i].start()
+    for copy in outward:
+        copy.wait()
 
 
 def shards(n_e, n_dp, tokens, routes, probs, cotangent, w_gate, w_up, w_down):
@@ -422,12 +506,12 @@
     dma = pltpu.SemaphoreType.DMA
     grad = jax.ShapeDtypeStruct((el, chunk, hid), BF)
     V = pltpu.VMEM
-    return pl.pallas_call(
+    results = pl.pallas_call(
         functools.partial(layer_kernel, n_e, n_dp),
         out_shape=(
             jax.ShapeDtypeStruct((t_n, width), BF),
             jax.ShapeDtypeStruct((t_n, width), BF),
-            jax.ShapeDtypeStruct(probs.shape, F32),
+            jax.ShapeDtypeStruct(probs.shape[::-1], F32),
             grad, grad, grad,
         ),
         in_specs=[vmem] * 7 + [hbm] * 3,
@@ -440,10 +524,20 @@
         + [V((3, n_dp, groups, el * msg, hid), BF)]
         + [V((n_dp, groups, el * msg, chunk), BF)] * 2
         + [V((el, groups * msg, hid), F32)] * 2
-        + [dma((3,)), dma((4,)), dma((3,)), dma((4, n_e)), dma((4, n_e)),
-           dma((2, groups, n_dp)), dma((2, groups, n_dp)), dma((3, n_dp)), dma((3, n_dp))],
+        + [dma((3,)), dma((4, 2)), dma((3,)), dma((4, 2, n_e)), dma((4, 2, n_e)),
+           dma((2, groups, 2, n_dp)), dma((2, groups, 2, n_dp))] + [dma((3, 2))] * 4,
         compiler_params=pltpu.CompilerParams(collective_id=0, has_side_effects=True, vmem_limit_bytes=67043328),
-    )(tokens, cotangent, routes, probs, jnp.asarray(col), jnp.asarray(row), jnp.asarray(perm), w_gate, w_up, w_down)
+    )(tokens, cotangent, routes.T, probs.T, jnp.asarray(col), jnp.asarray(row), jnp.asarray(perm), w_gate, w_up, w_down)
+    shapes = [jax.ShapeDtypeStruct(r.shape, r.dtype) for r in results]
+    count = len(shapes)
+    mixed, tgrad, pgrad, *grads = pl.pallas_call(
+        hand_out,
+        out_shape=shapes,
+        in_specs=[hbm] * count,
+        out_specs=[hbm] * count,
+        scratch_shapes=[V(r.shape, r.dtype) for r in shapes] + [dma((2, count))],
+    )(*results)
+    return mixed, tgrad, pgrad.T, *grads
 
 
 def solution(mesh):

time: 195 us -> 160 us (0.82); the launches traced: 192 us -> 160 us
  Pallas kernels: 178 us -> 160 us
  local copies, waits for them, and re-layouts: 13.5 us -> 0 us
    pallas_call x1, Pallas kernels: 178 us -> 155 us  [shards(): pl.pallas_call(functools.partial(layer_kernel, n_e, n_dp), out_shape=(jax...]
    unnamed x11 -> x0, local copies, waits for them, and re-layouts: 12.1 us -> none
    pallas_call x0 -> x1, Pallas kernels: none -> 4.38 us  [shards(): pl.pallas_call(hand_out, out_shape=shapes, in_specs=[hbm] * count, out_sp...]
where the time goes in v2:
time: 160 us
  Pallas kernels  160 us (100%)
    pallas_call x1, Pallas kernels, shards(): pl.pallas_call(functools.partial(layer_kernel, n_e, n_dp), out_shape=(jax...  155 us
    pallas_call x1, Pallas kernels, shards(): pl.pallas_call(hand_out, out_shape=shapes, in_specs=[hbm] * count, out_sp...  4.38 us

profile of v2, /device:TPU:7, one launch (start us, length us, event | category | flops | bytes accessed | tf_op | source)
XLA Modules:
  0.0 160.3 jit_solution(4085310476272945746)
XLA Ops:
  0.6 155.2 %shard_map.145 = (bf16[64,2048]{1,0:T(8,128)(2,1)}, bf16[64,2048]{1,0:T(8,128)(2,1)}, f32[8,64]{1,0:T(8,128)}, bf16[4,512,384]{2,1,0:T(8,128)(2,1)}, bf16[4,512,...) custom-call(bf16[64,2048]{1,0:T(8,128)(2,1)} %tok_ref.1, bf16[64,2048]{1,0:T(8,128)(2,1)} %cot_ref.1, s32[8,64]{1,0:T(8,128)} %bitcast.3, ...), custom_call_target="tpu_custom_call" | custom-call | tf_op jit(solution)/shard_map/pallas_call | solution.py:509
  155.8 4.4 %shard_map.146 = (bf16[64,2048]{1,0:T(8,128)(2,1)}, bf16[64,2048]{1,0:T(8,128)(2,1)}, f32[8,64]{1,0:T(8,128)}, bf16[4,512,384]{2,1,0:T(8,128)(2,1)}, bf16[4,512,...) custom-call(bf16[64,2048]{1,0:T(8,128)(2,1)} %get-tuple-element.18.refs_0_, bf16[64,2048]{1,0:T(8,128)(2,1)} %get-tuple-element.19.refs_1_, ...), custom_call_target="tpu_custom_call" | custom-call | tf_op jit(solution)/shard_map/pallas_call | solution.py:533

commit v3 on v2

--- a/solution.py
+++ b/solution.py
@@ -23,10 +23,11 @@
 
 def layer_kernel(
     n_e, n_dp,
-    tok_ref, cot_ref, routes_ref, probs_ref, col_ref, row_ref, perm_ref, wg_hbm, wu_hbm, wd_hbm,
+    tok_in, cot_in, routes_in, probs_in, col_in, row_in, perm_in, wg_hbm, wu_hbm, wd_hbm,
     mixed_ref, tgrad_ref, pgrad_ref, gg_hbm, gu_hbm, gd_hbm,
     sa, sb, ra, rb, ro, rd, x, u, q, g, gt, whi, wlo, wg, wu, wd, h, xs, us, pre_g, pre_u,
-    w_sem, loc_sem, out_sem, snd, rcv, ysnd_r, yrcv_r, ysnd_h, yrcv_h, ysnd_f, yrcv_f,
+    tok_ref, cot_ref, routes_ref, probs_ref, col_ref, row_ref, perm_ref,
+    in_sem, w_sem, loc_sem, out_sem, snd, rcv, ysnd_r, yrcv_r, ysnd_h, yrcv_h, ysnd_f, yrcv_f,
 ):
     me = lax.axis_index("expert")
     my = lax.axis_index("dp")
@@ -44,21 +45,30 @@
     gd = 4
     gb = gd * msg
 
+    barrier = pltpu.get_barrier_semaphore()
+
+    @pl.loop(1, n_e)
+    def _(d):
+        pl.semaphore_signal(barrier, inc=1, device_id={"expert": lax.rem(me + d, n_e)}, device_id_type=MESH)
+
+    for d in range(1, n_dp):
+        pl.semaphore_signal(barrier, inc=1, device_id={"dp": lax.rem(my + d, n_dp)}, device_id_type=MESH)
+
+    in_copies = [
+        pltpu.make_async_copy(src, dst, in_sem.at[i])
+        for i, (src, dst) in enumerate((
+            (routes_in, routes_ref), (probs_in, probs_ref), (col_in, col_ref), (tok_in, tok_ref),
+            (cot_in, cot_ref), (row_in, row_ref), (perm_in, perm_ref),
+        ))
+    ]
     w_copies = [
         pltpu.make_async_copy(src, dst, w_sem.at[i])
         for i, (src, dst) in enumerate(((wg_hbm, wg), (wu_hbm, wu), (wd_hbm, wd)))
     ]
-    for copy in w_copies:
+    for copy in in_copies + w_copies:
         copy.start()
-
-    barrier = pltpu.get_barrier_semaphore()
-
-    @pl.loop(1, n_e)
-    def _(d):
-        pl.semaphore_signal(barrier, inc=1, device_id={"expert": lax.rem(me + d, n_e)}, device_id_type=MESH)
-
-    for d in range(1, n_dp):
-        pl.semaphore_signal(barrier, inc=1, device_id={"dp": lax.rem(my + d, n_dp)}, device_id_type=MESH)
+    for copy in in_copies[:4]:
+        copy.wait()
 
     def eye(n):
         return jnp.where(
@@ -86,9 +96,6 @@
     place_c = jnp.concatenate([place] * n_dp, axis=0)
     share_c = jnp.concatenate([share_x] * n_dp, axis=0)
     tok_c = jnp.concatenate([tok_ref[:, c * chunk : (c + 1) * chunk] for c in range(n_dp)], axis=0)
-    cot_c = jnp.concatenate([cot_ref[:, c * chunk : (c + 1) * chunk] for c in range(n_dp)], axis=0)
-
-    pl.semaphore_wait(barrier, n_e - 1 + n_dp - 1)
 
     lane_e = lax.broadcasted_iota(jnp.int32, (gb, n_x), 1)
     lane_c = lax.broadcasted_iota(jnp.int32, (gb, n_dp * t_n), 1) // t_n
@@ -97,25 +104,27 @@
     col_c = col_ref[:, 2:3]
     n_g = n_e // gd
 
-    halves = 2
-    hw = chunk // halves
-
-    def message(buf, i, hf=None):
-        rows = pl.ds(pl.multiple_of(i * msg, msg), msg)
-        return buf.at[rows] if hf is None else buf.at[rows, pl.ds(hf * hw, hw)]
+    pieces = (4, 2, 2, 2)
+
+    def span(kind, hf):
+        wide = chunk // pieces[kind]
+        return pl.ds(hf * wide, wide)
+
+    def message(kind, buf, i, hf):
+        return buf.at[pl.ds(pl.multiple_of(i * msg, msg), msg), span(kind, hf)]
 
     def send(kind, src, dst, o, hf):
         @pl.when(o != me)
         def _():
             pltpu.make_async_remote_copy(
-                src_ref=message(src, o, hf), dst_ref=message(dst, me, hf),
+                src_ref=message(kind, src, o, hf), dst_ref=message(kind, dst, me, hf),
                 send_sem=snd.at[kind, hf, o], recv_sem=rcv.at[kind, hf, me],
                 device_id={"expert": o}, device_id_type=MESH,
             ).start()
 
         @pl.when(o == me)
         def _():
-            pltpu.make_async_copy(message(src, o, hf), message(dst, o, hf), loc_sem.at[kind, hf]).start()
+            pltpu.make_async_copy(message(kind, src, o, hf), message(kind, dst, o, hf), loc_sem.at[kind, hf]).start()
 
     def send_all(kind, src, dst, hf):
         @pl.loop(0, 8)
@@ -130,23 +139,23 @@
         @pl.when(i != me)
         def _():
             pltpu.make_async_remote_copy(
-                src_ref=message(dst, i, hf), dst_ref=message(dst, i, hf),
+                src_ref=message(kind, dst, i, hf), dst_ref=message(kind, dst, i, hf),
                 send_sem=snd.at[kind, hf, i], recv_sem=rcv.at[kind, hf, i],
                 device_id={"expert": i}, device_id_type=MESH,
             ).wait_recv()
 
         @pl.when(i == me)
         def _():
-            pltpu.make_async_copy(message(dst, i, hf), message(dst, i, hf), loc_sem.at[kind, hf]).wait()
+            pltpu.make_async_copy(message(kind, dst, i, hf), message(kind, dst, i, hf), loc_sem.at[kind, hf]).wait()
 
     def await_sent(kind, src):
         @pl.loop(0, n_e)
         def _(o):
             @pl.when(o != me)
             def _():
-                for hf in range(halves):
+                for hf in range(pieces[kind]):
                     pltpu.make_async_remote_copy(
-                        src_ref=message(src, o, hf), dst_ref=message(src, o, hf),
+                        src_ref=message(kind, src, o, hf), dst_ref=message(kind, src, o, hf),
                         send_sem=snd.at[kind, hf, o], recv_sem=rcv.at[kind, hf, o],
                         device_id={"expert": o}, device_id_type=MESH,
                     ).wait_send()
@@ -167,10 +176,14 @@
         chosen = jnp.where((held == col_s) & (lane_c == col_c), 1.0, 0.0).astype(BF)
         g[rows, :] = chosen
         sa[rows, :] = mm(chosen, tok_c).astype(BF)
-        for k in range(gd):
-            send(0, sa, ra, og * gd + k, 0)
-
-    send_all(0, sa, ra, 1)
+
+    pl.semaphore_wait(barrier, n_e - 1 + n_dp - 1)
+    for hf in range(pieces[0]):
+        send_all(0, sa, ra, hf)
+
+    for copy in in_copies[4:]:
+        copy.wait()
+    cot_c = jnp.concatenate([cot_ref[:, c * chunk : (c + 1) * chunk] for c in range(n_dp)], axis=0)
 
     @pl.loop(0, n_g)
     def _(i):
@@ -203,15 +216,14 @@
         whi[:, cols] = high
         wlo[:, cols] = (weight - high.astype(F32)).astype(BF)
 
-    def regroup(dst_write, src, gr, hf):
-        cols = slice(0, chunk) if hf is None else slice(hf * hw, (hf + 1) * hw)
+    def regroup(dst_write, src, gr, cols):
         for p in range(2):
             dst_write(p, mm(q[p * half : (p + 1) * half, :], src[gr * grows : (gr + 1) * grows, cols]).astype(BF))
 
     ex_rows = el * per
 
     def y_rows(kind, src, dst, gr, hf):
-        cols = pl.ds(hf * hw, hw)
+        cols = span(kind, hf)
         for d in (1, n_dp - 1, 2):
             to = lax.rem(my + d, n_dp)
             pltpu.make_async_remote_copy(
@@ -224,7 +236,7 @@
         ).start()
 
     def y_rows_wait(kind, src, dst, gr, hf):
-        cols = pl.ds(hf * hw, hw)
+        cols = span(kind, hf)
         for d in range(1, n_dp):
             frm = lax.rem(my + d, n_dp)
             pltpu.make_async_remote_copy(
@@ -268,18 +280,16 @@
                 device_id={"dp": sides[i]}, device_id_type=MESH,
             ).wait_recv()
 
-    def into(dst, gr, hf):
-        cols = slice(hf * hw, (hf + 1) * hw)
-
+    def into(dst, gr, cols):
         def write(p, value):
             for c in range(n_dp // 2):
                 dst[gr, p * (n_dp // 2) + c, :, cols] = value[c * ex_rows : (c + 1) * ex_rows]
         return write
 
-    for hf in range(halves):
+    for hf in range(pieces[0]):
         await_all(0, ra, hf)
         for gr in range(groups):
-            regroup(into(x, gr, hf), ra, gr, hf)
+            regroup(into(x, gr, span(0, hf)), ra, gr, span(0, hf))
             y_rows(0, x, xs, gr, hf)
 
     def rows_of(src, c, e):
@@ -321,14 +331,14 @@
         return write
 
     for gr in range(groups):
-        regroup(plain(sa, gr), ra, gr, None)
-    for hf in range(halves):
+        regroup(plain(sa, gr), ra, gr, slice(0, chunk))
+    for hf in range(pieces[2]):
         send_all(2, sa, ro, hf)
 
-    for hf in range(halves):
+    for hf in range(pieces[1]):
         await_all(1, rb, hf)
         for gr in range(groups):
-            regroup(into(u, gr, hf), rb, gr, hf)
+            regroup(into(u, gr, span(1, hf)), rb, gr, span(1, hf))
         if hf == 0:
             hand_on(0, 0)
             hand_on(0, 1)
@@ -355,11 +365,11 @@
     y_hidden(2)
     await_sent(1, sb)
     for gr in range(groups):
-        regroup(plain(sb, gr), rb, gr, None)
-    for hf in range(halves):
+        regroup(plain(sb, gr), rb, gr, slice(0, chunk))
+    for hf in range(pieces[3]):
         send_all(3, sb, rd, hf)
 
-    for hf in range(halves):
+    for hf in range(pieces[2]):
         await_all(2, ro, hf)
     mixed = mm(whi[...], ro[...]) + mm(wlo[...], ro[...])
     for c in range(n_dp):
@@ -398,10 +408,10 @@
         )
 
     y_hidden_far(0)
-    for hf in range(halves):
-        for gr in range(groups):
-            y_rows_wait(1, u, us, gr, hf)
-            y_rows_wait(0, x, xs, gr, hf)
+    for kind, (src, dst) in enumerate(((x, xs), (u, us))):
+        for hf in range(pieces[kind]):
+            for gr in range(groups):
+                y_rows_wait(kind, src, dst, gr, hf)
 
     @pl.loop(0, el)
     def _(e):
@@ -414,7 +424,7 @@
         hand_on(kind, 0)
         hand_on(kind, 1)
 
-    for hf in range(halves):
+    for hf in range(pieces[3]):
         await_all(3, rd, hf)
     tgrad = mm(gt[...], rd[...])
     for c in range(n_dp):
@@ -443,8 +453,8 @@
         to = lax.rem(my + d, n_dp)
         for kind, (src, dst) in enumerate(((x, xs), (u, us))):
             for gr in range(groups):
-                for hf in range(halves):
-                    cols = pl.ds(hf * hw, hw)
+                for hf in range(pieces[kind]):
+                    cols = span(kind, hf)
                     pltpu.make_async_remote_copy(
                         src_ref=src.at[gr, to, :, cols], dst_ref=dst.at[my, gr, :, cols],
                         send_sem=ysnd_r.at[kind, gr, hf, d], recv_sem=yrcv_r.at[kind, gr, hf, my],
@@ -483,6 +493,7 @@
 
 def shards(n_e, n_dp, tokens, routes, probs, cotangent, w_gate, w_up, w_down):
     t_n, width = tokens.shape
+    top = routes.shape[1]
     el, _, hid = w_gate.shape
     chunk = width // n_dp
     blocks = n_dp * el
@@ -514,7 +525,7 @@
             jax.ShapeDtypeStruct(probs.shape[::-1], F32),
             grad, grad, grad,
         ),
-        in_specs=[vmem] * 7 + [hbm] * 3,
+        in_specs=[hbm] * 10,
         out_specs=[vmem] * 3 + [hbm] * 3,
         scratch_shapes=[V((slots, chunk), BF)] * 6
         + [V((groups, n_dp, el * msg, chunk), BF)] * 2
@@ -524,8 +535,11 @@
         + [V((3, n_dp, groups, el * msg, hid), BF)]
         + [V((n_dp, groups, el * msg, chunk), BF)] * 2
         + [V((el, groups * msg, hid), F32)] * 2
-        + [dma((3,)), dma((4, 2)), dma((3,)), dma((4, 2, n_e)), dma((4, 2, n_e)),
-           dma((2, groups, 2, n_dp)), dma((2, groups, 2, n_dp))] + [dma((3, 2))] * 4,
+        + [V(tokens.shape, BF)] * 2
+        + [V((top, t_n), jnp.int32), V((top, t_n), F32)]
+        + [V(a.shape, jnp.int32) for a in (col, row, perm)]
+        + [dma((7,)), dma((3,)), dma((4, 4)), dma((3,)), dma((4, 4, n_e)), dma((4, 4, n_e)),
+           dma((2, groups, 4, n_dp)), dma((2, groups, 4, n_dp))] + [dma((3, 2))] * 4,
         compiler_params=pltpu.CompilerParams(collective_id=0, has_side_effects=True, vmem_limit_bytes=67043328),
     )(tokens, cotangent, routes.T, probs.T, jnp.asarray(col), jnp.asarray(row), jnp.asarray(perm), w_gate, w_up, w_down)
     shapes = [jax.ShapeDtypeStruct(r.shape, r.dtype) for r in results]

time: 160 us -> 160 us (level)
  Pallas kernels: 160 us -> 158 us
where the time goes in v3:
time: 160 us; the launch traced here: 159 us
  Pallas kernels  158 us (99%)
    pallas_call x1, Pallas kernels, shards(): pl.pallas_call(functools.partial(layer_kernel, n_e, n_dp), out_shape=(jax...  154 us
    pallas_call x1, Pallas kernels, shards(): pl.pallas_call(hand_out, out_shape=shapes, in_specs=[hbm] * count, out_sp...  4.38 us

profile of v3, /device:TPU:7, one launch (start us, length us, event | category | flops | bytes accessed | tf_op | source)
XLA Modules:
  0.0 159.1 jit_solution(18313310897265364215)
XLA Ops:
  0.6 153.9 %shard_map.145 = (bf16[64,2048]{1,0:T(8,128)(2,1)}, bf16[64,2048]{1,0:T(8,128)(2,1)}, f32[8,64]{1,0:T(8,128)}, bf16[4,512,384]{2,1,0:T(8,128)(2,1)}, bf16[4,512,...) custom-call(bf16[64,2048]{1,0:T(8,128)(2,1)} %tok_in.1, bf16[64,2048]{1,0:T(8,128)(2,1)} %cot_in.1, s32[8,64]{1,0:T(8,128)} %bitcast.3, ...), custom_call_target="tpu_custom_call" | custom-call | tf_op jit(solution)/shard_map/pallas_call | solution.py:520
  154.5 4.4 %shard_map.146 = (bf16[64,2048]{1,0:T(8,128)(2,1)}, bf16[64,2048]{1,0:T(8,128)(2,1)}, f32[8,64]{1,0:T(8,128)}, bf16[4,512,384]{2,1,0:T(8,128)(2,1)}, bf16[4,512,...) custom-call(bf16[64,2048]{1,0:T(8,128)(2,1)} %get-tuple-element.18.refs_0_, bf16[64,2048]{1,0:T(8,128)(2,1)} %get-tuple-element.19.refs_1_, ...), custom_call_target="tpu_custom_call" | custom-call | tf_op jit(solution)/shard_map/pallas_call | solution.py:547

commit v4 on v3

--- a/solution.py
+++ b/solution.py
@@ -27,7 +27,7 @@
     mixed_ref, tgrad_ref, pgrad_ref, gg_hbm, gu_hbm, gd_hbm,
     sa, sb, ra, rb, ro, rd, x, u, q, g, gt, whi, wlo, wg, wu, wd, h, xs, us, pre_g, pre_u,
     tok_ref, cot_ref, routes_ref, probs_ref, col_ref, row_ref, perm_ref,
-    in_sem, w_sem, loc_sem, out_sem, snd, rcv, ysnd_r, yrcv_r, ysnd_h, yrcv_h, ysnd_f, yrcv_f,
+    in_sem, w_sem, loc_sem, out_sem, snd, rcv, ysnd_r, yrcv_r, y_loc, ysnd_h, yrcv_h, ysnd_f, yrcv_f,
 ):
     me = lax.axis_index("expert")
     my = lax.axis_index("dp")
@@ -65,10 +65,12 @@
         pltpu.make_async_copy(src, dst, w_sem.at[i])
         for i, (src, dst) in enumerate(((wg_hbm, wg), (wu_hbm, wu), (wd_hbm, wd)))
     ]
-    for copy in in_copies + w_copies:
+    for copy in in_copies[:4]:
         copy.start()
     for copy in in_copies[:4]:
         copy.wait()
+    for copy in in_copies[4:] + w_copies:
+        copy.start()
 
     def eye(n):
         return jnp.where(
@@ -113,18 +115,22 @@
     def message(kind, buf, i, hf):
         return buf.at[pl.ds(pl.multiple_of(i * msg, msg), msg), span(kind, hf)]
 
+    def own(buf):
+        return buf.at[pl.ds(pl.multiple_of(me * msg, msg), msg)]
+
     def send(kind, src, dst, o, hf):
         @pl.when(o != me)
         def _():
             pltpu.make_async_remote_copy(
                 src_ref=message(kind, src, o, hf), dst_ref=message(kind, dst, me, hf),
-                send_sem=snd.at[kind, hf, o], recv_sem=rcv.at[kind, hf, me],
+                send_sem=snd.at[kind], recv_sem=rcv.at[kind, hf],
                 device_id={"expert": o}, device_id_type=MESH,
             ).start()
 
-        @pl.when(o == me)
-        def _():
-            pltpu.make_async_copy(message(kind, src, o, hf), message(kind, dst, o, hf), loc_sem.at[kind, hf]).start()
+        if hf == 0:
+            @pl.when(o == me)
+            def _():
+                pltpu.make_async_copy(own(src), own(dst), loc_sem.at[kind]).start()
 
     def send_all(kind, src, dst, hf):
         @pl.loop(0, 8)
@@ -135,38 +141,28 @@
             for dx in (2, 1, 3, 0):
                 send(kind, src, dst, z * 8 + lax.rem(me // 2 + dx, 4) * 2 + core, hf)
 
-    def await_from(kind, dst, i, hf):
-        @pl.when(i != me)
-        def _():
-            pltpu.make_async_remote_copy(
-                src_ref=message(kind, dst, i, hf), dst_ref=message(kind, dst, i, hf),
-                send_sem=snd.at[kind, hf, i], recv_sem=rcv.at[kind, hf, i],
-                device_id={"expert": i}, device_id_type=MESH,
-            ).wait_recv()
-
-        @pl.when(i == me)
-        def _():
-            pltpu.make_async_copy(message(kind, dst, i, hf), message(kind, dst, i, hf), loc_sem.at[kind, hf]).wait()
+    others = (n_e - 1) * msg
 
     def await_sent(kind, src):
-        @pl.loop(0, n_e)
-        def _(o):
-            @pl.when(o != me)
-            def _():
-                for hf in range(pieces[kind]):
-                    pltpu.make_async_remote_copy(
-                        src_ref=message(kind, src, o, hf), dst_ref=message(kind, src, o, hf),
-                        send_sem=snd.at[kind, hf, o], recv_sem=rcv.at[kind, hf, o],
-                        device_id={"expert": o}, device_id_type=MESH,
-                    ).wait_send()
+        part = src.at[0:others]
+        pltpu.make_async_remote_copy(
+            src_ref=part, dst_ref=part, send_sem=snd.at[kind], recv_sem=rcv.at[kind, 0],
+            device_id={"dp": my}, device_id_type=MESH,
+        ).wait_send()
 
     def await_all(kind, dst, hf):
-        @pl.loop(0, n_e)
-        def _(i):
-            await_from(kind, dst, i, hf)
+        part = dst.at[0:others, span(kind, hf)]
+        pltpu.make_async_remote_copy(
+            src_ref=part, dst_ref=part, send_sem=snd.at[kind], recv_sem=rcv.at[kind, hf],
+            device_id={"dp": my}, device_id_type=MESH,
+        ).wait_recv()
+        if hf == 0:
+            pltpu.make_async_copy(own(dst), own(dst), loc_sem.at[kind]).wait()
 
     def pick(og):
         return jnp.where(lane_e == col_e + og * (gd * el), 1.0, 0.0)
+
+    pl.semaphore_wait(barrier, n_e - 1 + n_dp - 1)
 
     @pl.loop(0, n_g)
     def _(i):
@@ -176,9 +172,10 @@
         chosen = jnp.where((held == col_s) & (lane_c == col_c), 1.0, 0.0).astype(BF)
         g[rows, :] = chosen
         sa[rows, :] = mm(chosen, tok_c).astype(BF)
-
-    pl.semaphore_wait(barrier, n_e - 1 + n_dp - 1)
-    for hf in range(pieces[0]):
+        for k in range(gd):
+            send(0, sa, ra, og * gd + k, 0)
+
+    for hf in range(1, pieces[0]):
         send_all(0, sa, ra, hf)
 
     for copy in in_copies[4:]:
@@ -228,25 +225,21 @@
             to = lax.rem(my + d, n_dp)
             pltpu.make_async_remote_copy(
                 src_ref=src.at[gr, to, :, cols], dst_ref=dst.at[my, gr, :, cols],
-                send_sem=ysnd_r.at[kind, gr, hf, d], recv_sem=yrcv_r.at[kind, gr, hf, my],
+                send_sem=ysnd_r.at[kind], recv_sem=yrcv_r.at[kind],
                 device_id={"dp": to}, device_id_type=MESH,
             ).start()
-        pltpu.make_async_copy(
-            src.at[gr, my, :, cols], dst.at[my, gr, :, cols], yrcv_r.at[kind, gr, hf, my]
-        ).start()
-
-    def y_rows_wait(kind, src, dst, gr, hf):
-        cols = span(kind, hf)
-        for d in range(1, n_dp):
-            frm = lax.rem(my + d, n_dp)
-            pltpu.make_async_remote_copy(
-                src_ref=src.at[gr, frm, :, cols], dst_ref=dst.at[frm, gr, :, cols],
-                send_sem=ysnd_r.at[kind, gr, hf, d], recv_sem=yrcv_r.at[kind, gr, hf, frm],
-                device_id={"dp": frm}, device_id_type=MESH,
-            ).wait_recv()
-        pltpu.make_async_copy(
-            src.at[gr, my, :, cols], dst.at[my, gr, :, cols], yrcv_r.at[kind, gr, hf, my]
-        ).wait()
+        pltpu.make_async_copy(src.at[gr, my, :, cols], dst.at[my, gr, :, cols], y_loc.at[kind]).start()
+
+    def y_rows_done(kind, dst):
+        part = dst.at[0 : n_dp - 1]
+        return pltpu.make_async_remote_copy(
+            src_ref=part, dst_ref=part, send_sem=ysnd_r.at[kind], recv_sem=yrcv_r.at[kind],
+            device_id={"expert": me}, device_id_type=MESH,
+        )
+
+    def y_rows_wait(kind, dst):
+        y_rows_done(kind, dst).wait_recv()
+        pltpu.make_async_copy(dst.at[my], dst.at[my], y_loc.at[kind]).wait()
 
     far = lax.rem(my + 2, n_dp)
     sides = (lax.rem(my + 1, n_dp), lax.rem(my + n_dp - 1, n_dp))
@@ -408,10 +401,8 @@
         )
 
     y_hidden_far(0)
-    for kind, (src, dst) in enumerate(((x, xs), (u, us))):
-        for hf in range(pieces[kind]):
-            for gr in range(groups):
-                y_rows_wait(kind, src, dst, gr, hf)
+    y_rows_wait(0, xs)
+    y_rows_wait(1, us)
 
     @pl.loop(0, el)
     def _(e):
@@ -423,6 +414,23 @@
     for kind in (1, 2):
         hand_on(kind, 0)
         hand_on(kind, 1)
+
+    y_hidden_far(1)
+
+    @pl.loop(0, el)
+    def _(e):
+        wg[e, 0 * chunk : 1 * chunk, :] = mm(gathered(xs, e), hidden_of(1, e), TN).astype(BF)
+
+    out_g = pltpu.make_async_copy(wg.at[:, 0 * chunk : 1 * chunk], gg_hbm, out_sem.at[0])
+    out_g.start()
+    y_hidden_far(2)
+
+    @pl.loop(0, el)
+    def _(e):
+        wg[e, 1 * chunk : 2 * chunk, :] = mm(gathered(xs, e), hidden_of(2, e), TN).astype(BF)
+
+    out_u = pltpu.make_async_copy(wg.at[:, 1 * chunk : 2 * chunk], gu_hbm, out_sem.at[1])
+    out_u.start()
 
     for hf in range(pieces[3]):
         await_all(3, rd, hf)
@@ -430,36 +438,10 @@
     for c in range(n_dp):
         tgrad_ref[:, c * chunk : (c + 1) * chunk] = tgrad[c * t_n : (c + 1) * t_n].astype(BF)
 
-    y_hidden_far(1)
-
-    @pl.loop(0, el)
-    def _(e):
-        wg[e, 0 * chunk : 1 * chunk, :] = mm(gathered(xs, e), hidden_of(1, e), TN).astype(BF)
-
-    out_g = pltpu.make_async_copy(wg.at[:, 0 * chunk : 1 * chunk], gg_hbm, out_sem.at[0])
-    out_g.start()
-    y_hidden_far(2)
-
-    @pl.loop(0, el)
-    def _(e):
-        wg[e, 1 * chunk : 2 * chunk, :] = mm(gathered(xs, e), hidden_of(2, e), TN).astype(BF)
-
-    out_u = pltpu.make_async_copy(wg.at[:, 1 * chunk : 2 * chunk], gu_hbm, out_sem.at[1])
-    out_u.start()
-
     await_sent(2, sa)
     await_sent(3, sb)
-    for d in range(1, n_dp):
-        to = lax.rem(my + d, n_dp)
-        for kind, (src, dst) in enumerate(((x, xs), (u, us))):
-            for gr in range(groups):
-                for hf in range(pieces[kind]):
-                    cols = span(kind, hf)
-                    pltpu.make_async_remote_copy(
-                        src_ref=src.at[gr, to, :, cols], dst_ref=dst.at[my, gr, :, cols],
-                        send_sem=ysnd_r.at[kind, gr, hf, d], recv_sem=yrcv_r.at[kind, gr, hf, my],
-                        device_id={"dp": to}, device_id_type=MESH,
-                    ).wait_send()
+    y_rows_done(0, xs).wait_send()
+    y_rows_done(1, us).wait_send()
     for kind in range(3):
         for i in range(2):
             pltpu.make_async_remote_copy(
@@ -480,13 +462,17 @@
 def hand_out(*refs):
     count = (len(refs) - 1) // 3
     srcs, dsts, held, sem = refs[:count], refs[count : 2 * count], refs[2 * count : 3 * count], refs[-1]
-    inward = [pltpu.make_async_copy(srcs[i], held[i], sem.at[0, i]) for i in range(count)]
-    outward = [pltpu.make_async_copy(held[i], dsts[i], sem.at[1, i]) for i in range(count)]
+    inward, outward = [], []
+    for i in list(range(3, count)) + [0, 1, 2]:
+        for at in (range(srcs[i].shape[0]) if i > 2 else [slice(None)]):
+            n = len(inward)
+            inward.append(pltpu.make_async_copy(srcs[i].at[at], held[i].at[at], sem.at[0, n]))
+            outward.append(pltpu.make_async_copy(held[i].at[at], dsts[i].at[at], sem.at[1, n]))
     for copy in inward:
         copy.start()
-    for i in range(count):
-        inward[i].wait()
-        outward[i].start()
+    for into, out in zip(inward, outward):
+        into.wait()
+        out.start()
     for copy in outward:
         copy.wait()
 
@@ -538,8 +524,7 @@
         + [V(tokens.shape, BF)] * 2
         + [V((top, t_n), jnp.int32), V((top, t_n), F32)]
         + [V(a.shape, jnp.int32) for a in (col, row, perm)]
-        + [dma((7,)), dma((3,)), dma((4, 4)), dma((3,)), dma((4, 4, n_e)), dma((4, 4, n_e)),
-           dma((2, groups, 4, n_dp)), dma((2, groups, 4, n_dp))] + [dma((3, 2))] * 4,
+        + [dma((7,)), dma((3,)), dma((4,)), dma((3,)), dma((4,)), dma((4, 4)), dma((2,)), dma((2,)), dma((2,))] + [dma((3, 2))] * 4,
         compiler_params=pltpu.CompilerParams(collective_id=0, has_side_effects=True, vmem_limit_bytes=67043328),
     )(tokens, cotangent, routes.T, probs.T, jnp.asarray(col), jnp.asarray(row), jnp.asarray(perm), w_gate, w_up, w_down)
     shapes = [jax.ShapeDtypeStruct(r.shape, r.dtype) for r in results]
@@ -549,7 +534,7 @@
         out_shape=shapes,
         in_specs=[hbm] * count,
         out_specs=[hbm] * count,
-        scratch_shapes=[V(r.shape, r.dtype) for r in shapes] + [dma((2, count))],
+        scratch_shapes=[V(r.shape, r.dtype) for r in shapes] + [dma((2, 3 + 3 * el))],
     )(*results)
     return mixed, tgrad, pgrad.T, *grads
 

time: 160 us -> 148 us (0.925)
  Pallas kernels: 158 us -> 147 us
    pallas_call x1, Pallas kernels: 154 us -> 143 us  [shards(): pl.pallas_call(functools.partial(layer_kernel, n_e, n_dp), out_shape=(jax...]
where the time goes in v4:
time: 148 us
  Pallas kernels  147 us (99%)
    pallas_call x1, Pallas kernels, shards(): pl.pallas_call(functools.partial(layer_kernel, n_e, n_dp), out_shape=(jax...  143 us
    pallas_call x1, Pallas kernels, shards(): pl.pallas_call(hand_out, out_shape=shapes, in_specs=[hbm] * count, out_sp...  4.82 us

profile of v4, /device:TPU:7, one launch (start us, length us, event | category | flops | bytes accessed | tf_op | source)
XLA Modules:
  0.0 148.2 jit_solution(18042437262232917406)
XLA Ops:
  0.6 142.6 %shard_map.145 = (bf16[64,2048]{1,0:T(8,128)(2,1)}, bf16[64,2048]{1,0:T(8,128)(2,1)}, f32[8,64]{1,0:T(8,128)}, bf16[4,512,384]{2,1,0:T(8,128)(2,1)}, bf16[4,512,...) custom-call(bf16[64,2048]{1,0:T(8,128)(2,1)} %tok_in.1, bf16[64,2048]{1,0:T(8,128)(2,1)} %cot_in.1, s32[8,64]{1,0:T(8,128)} %bitcast.3, ...), custom_call_target="tpu_custom_call" | custom-call | tf_op jit(solution)/shard_map/pallas_call | solution.py:506
  143.2 4.8 %shard_map.146 = (bf16[64,2048]{1,0:T(8,128)(2,1)}, bf16[64,2048]{1,0:T(8,128)(2,1)}, f32[8,64]{1,0:T(8,128)}, bf16[4,512,384]{2,1,0:T(8,128)(2,1)}, bf16[4,512,...) custom-call(bf16[64,2048]{1,0:T(8,128)(2,1)} %get-tuple-element.18.refs_0_, bf16[64,2048]{1,0:T(8,128)(2,1)} %get-tuple-element.19.refs_1_, ...), custom_call_target="tpu_custom_call" | custom-call | tf_op jit(solution)/shard_map/pallas_call | solution.py:532
